TPU v7x, 256 devices: a whole 4x4x8 slice. The times are simulated.
256 devices in a mesh: tm: 64 (over z_lo, y, x), space: 4 (over z_hi, core).
Axes of the slice: x: 4, y: 4, z: 8 (z_hi: 2, z_lo: 4; z = z_hi * 4 + z_lo), core: 2. Of those that a mesh axis runs over, the one named last changes fastest.
Arguments:
- state_field: float32 [128, 16, 16, 128], P('tm', 'space'), may hold values from -3 to 3
- adjoint: float32 [128, 16, 16, 128], P('tm', 'space'), may hold values from -3 to 3
- target: float32 [128, 16, 16, 128], P('tm', 'space'), may hold values from -4 to 4
- initial_state: float32 [16, 16, 128], P('space'), may hold values from -4 to 4
- conductivity: float32 [16, 16, 128], P('space'), may hold values from 0.05 to 0.5
- reaction: float32 [16, 16, 128], P('space'), may hold values from 0.05 to 1
Outputs:
- new_state: float32 [128, 16, 16, 128], P('tm', 'space')
- new_adjoint: float32 [128, 16, 16, 128], P('tm', 'space')
All inputs are finite; a program needn't handle non-finite values.
Results may differ from a plain program's by a relative error of at most 0.00029.
Values sent between devices are 32-bit elements; how exact they have to be, the bound alone decides.
No kernel may reach another device: no remote copies, remote signals or barrier semaphores. Data moves between devices by JAX's collectives and lax.ppermute only.
A program may use at most 64 MiB of HBM per device.

v0:
```python
import math

import jax
import jax.numpy as jnp
from jax import lax
from jax.sharding import PartitionSpec as P

CHEB = 8


highest = lax.Precision.HIGHEST
step_rate = 2.0
coupling = 1.0
lower_edge = 0.05
upper_edge = 7.0


def from_behind(value, axis, steps):
    count = lax.axis_size(axis)
    leading, last = (max(0, -steps), min(count, count - steps))
    return lax.ppermute(value, axis, [(source, source + steps) for source in range(leading, last)])


def padded(block, sides, width):
    for axis, dim in sides:
        count = lax.axis_size(axis)
        forward = [(i, i + 1) for i in range(count - 1)]
        backward = [(target, source) for source, target in forward]
        low = lax.ppermute(
            lax.slice_in_dim(block, block.shape[dim] - width, None, axis=dim), axis, forward
        )
        high = lax.ppermute(lax.slice_in_dim(block, 0, width, axis=dim), axis, backward)
        block = jnp.concatenate([low, block, high], axis=dim)
    return block


def in_one_piece(arrays, axis, dim, along):
    both = jnp.concatenate(arrays, axis=along)
    filled, at, finished = (lax.all_gather(both, axis, axis=dim, tiled=True), 0, [])
    for a in arrays:
        finished.append(lax.slice_in_dim(filled, at, at + a.shape[along], axis=along))
        at += a.shape[along]
    return tuple(finished)


def face_term(values, cond_mid, cond_axis):
    value_axis = values.ndim - 3 + cond_axis
    length = values.shape[value_axis]
    face_cond = 0.5 * (
        lax.slice_in_dim(cond_mid, 0, length - 1, axis=cond_axis)
        + lax.slice_in_dim(cond_mid, 1, length, axis=cond_axis)
    )
    flux = face_cond * (
        lax.slice_in_dim(values, 0, length - 1, axis=value_axis)
        - lax.slice_in_dim(values, 1, length, axis=value_axis)
    )
    zero_face = jnp.zeros_like(lax.slice_in_dim(flux, 0, 1, axis=value_axis))
    return jnp.concatenate([flux, zero_face], value_axis) - jnp.concatenate(
        [zero_face, flux], value_axis
    )


def lateral(centre, cond_mid):
    count_y = cond_mid.shape[1]
    count_z = cond_mid.shape[2]
    row_y = jnp.arange(count_y, dtype=jnp.int32)[:, None]
    row_z = jnp.arange(count_z, dtype=jnp.int32)[None, :]
    edges = (
        (row_y == 0).astype(jnp.float32)
        + (row_y == count_y - 1).astype(jnp.float32)
        + (row_z == 0).astype(jnp.float32)
        + (row_z == count_z - 1).astype(jnp.float32)
    )
    result = face_term(centre, cond_mid, 1) + face_term(centre, cond_mid, 2)
    return result + 0.5 * cond_mid * edges * centre


def diffusion(centre, below, above, cond_mid, cond_below, cond_above):
    result = lateral(centre, cond_mid)
    x_axis = centre.ndim - 3
    inner = 0.5 * (cond_mid[:-1] + cond_mid[1:]) * (centre[..., :-1, :, :] - centre[..., 1:, :, :])
    lower_face = 0.5 * (cond_mid[:1] + cond_below) * (below - centre[..., :1, :, :])
    upper_face = 0.5 * (cond_mid[-1:] + cond_above) * (centre[..., -1:, :, :] - above)
    faces = jnp.concatenate([lower_face, inner, upper_face], x_axis)
    return result + faces[..., 1:, :, :] - faces[..., :-1, :, :]


def edge_rows(values, depth, axis):
    length = values.shape[axis]
    return jnp.concatenate(
        [
            lax.slice_in_dim(values, 0, depth, axis=axis),
            lax.slice_in_dim(values, length - depth, length, axis=axis),
        ],
        axis,
    )


def unit_circle_arguments(mode_number, temporal_nodes, accumulated_sum):
    return (
        2.0
        * math.pi
        / accumulated_sum
        * (mode_number * temporal_nodes % accumulated_sum).astype(jnp.float32)
    )


def chebyshev(right_side, apply_system, lower_bound, upper_bound):
    centre_value = 0.5 * (upper_bound + lower_bound)
    half_width = 0.5 * (upper_bound - lower_bound)
    ratio_value = centre_value / half_width
    rho_now = 1.0 / ratio_value
    solution = jnp.zeros_like(right_side)
    residue = right_side
    direction = right_side / centre_value
    for repeat in range(CHEB):
        solution = solution + direction
        if repeat + 1 < CHEB:
            residue = residue - apply_system(direction)
            rho_next = 1.0 / (2.0 * ratio_value - rho_now)
            direction = rho_next * rho_now * direction + 2.0 * rho_next / half_width * residue
            rho_now = rho_next
    return solution


def shards(state_field, adjoint, target, initial_state, conductivity, reaction):
    local_steps, width_x, width_y, width_z = state_field.shape
    devices_time = lax.axis_size("tm")
    devices_space = lax.axis_size("space")
    horizon_length = local_steps * devices_time
    time_rank = lax.axis_index("tm")
    space_rank = lax.axis_index("space")
    cell_count = width_x * width_y * width_z
    earlier_last = from_behind(state_field[local_steps - 1], "tm", 1)
    earlier_last = jnp.where(time_rank == 0, initial_state, earlier_last)
    later_first = from_behind(adjoint[0], "tm", -1)
    preceding_iterate = jnp.concatenate([earlier_last[None], state_field[:-1]], 0)
    later_steps = jnp.concatenate([adjoint[1:], later_first[None]], 0)
    stacked = jnp.concatenate(
        [
            edge_rows(state_field, 1, 1),
            edge_rows(adjoint, 1, 1),
            edge_rows(conductivity, 1, 0)[None],
        ],
        0,
    )
    rims = padded(stacked, (("space", 1),), 1)
    below_all = rims[:, 0:1]
    above_all = rims[:, 3:4]
    cond_below = below_all[2 * local_steps]
    cond_above = above_all[2 * local_steps]
    diff_state = diffusion(
        state_field,
        below_all[:local_steps],
        above_all[:local_steps],
        conductivity,
        cond_below,
        cond_above,
    )
    diff_adjoint = diffusion(
        adjoint,
        below_all[local_steps : 2 * local_steps],
        above_all[local_steps : 2 * local_steps],
        conductivity,
        cond_below,
        cond_above,
    )
    state_res = (
        step_rate * (state_field - preceding_iterate)
        + diff_state
        + state_field * state_field * state_field / 3.0
        + coupling * adjoint
    )
    adjoint_res = (
        step_rate * (adjoint - later_steps)
        + diff_adjoint
        + state_field * state_field * adjoint
        - state_field
        + target
    )
    residual = jnp.stack([state_res, adjoint_res]).reshape(2, local_steps, cell_count)
    temporal_nodes = jnp.arange(horizon_length, dtype=jnp.int32)[None, :]
    slot_total = horizon_length // 2
    mode_number = jnp.arange(slot_total, dtype=jnp.int32)[:, None]
    diagonal_twist_weights = unit_circle_arguments(mode_number, temporal_nodes, horizon_length)
    cosine_table = jnp.cos(diagonal_twist_weights)
    sine_table = jnp.sin(diagonal_twist_weights)
    alternation = jnp.cos(
        unit_circle_arguments(horizon_length // 2, temporal_nodes, horizon_length)
    )
    forward = jnp.stack([cosine_table, jnp.where(mode_number == 0, alternation, -sine_table)])
    inverse = (
        jnp.stack(
            [
                jnp.where(mode_number == 0, 1.0, 2.0) * cosine_table,
                jnp.where(mode_number == 0, alternation, -2.0 * sine_table),
            ]
        )
        / horizon_length
    )
    slot_count = slot_total // devices_time
    slot_ids = time_rank * slot_count + jnp.arange(slot_count, dtype=jnp.int32)
    thetas = unit_circle_arguments(slot_ids, 1, horizon_length)
    shift_real = step_rate * (1.0 - jnp.cos(thetas))
    shift_imag = jnp.where(slot_ids == 0, 2.0 * step_rate, shift_real)
    twist_slot = step_rate * jnp.sin(thetas)
    spectral = jnp.einsum(
        "rkt,mtc->mrkc",
        forward,
        lax.all_to_all(residual, "tm", split_axis=2, concat_axis=1, tiled=True),
        precision=highest,
    )
    spectrum = lax.all_to_all(spectral, "tm", split_axis=2, concat_axis=3, tiled=True)
    fields = spectrum.reshape((2, 2, slot_count, width_x, width_y, width_z))
    item_total = 4 * slot_count
    item_share = item_total // devices_space
    flat_fields = fields.reshape(item_total, width_x, width_y, width_z)
    grids = lax.all_to_all(flat_fields, "space", split_axis=0, concat_axis=1, tiled=True)
    cond_full, react_full = in_one_piece((conductivity, reaction), "space", 0, 1)
    item_ids = space_rank * item_share + jnp.arange(item_share, dtype=jnp.int32)
    slot_of = item_ids % slot_count
    part_of = item_ids // slot_count % 2
    picker = (slot_of[:, None] == jnp.arange(slot_count, dtype=jnp.int32)[None, :]).astype(
        jnp.float32
    )
    pick_real = jnp.sum(picker * shift_real[None, :], 1)
    pick_imag = jnp.sum(picker * shift_imag[None, :], 1)
    pick_twist = jnp.sum(picker * twist_slot[None, :], 1)
    item_shift = jnp.where(part_of == 0, pick_real, pick_imag).reshape(item_share, 1, 1, 1)
    item_spread = (pick_twist * pick_twist + coupling).reshape(item_share, 1, 1, 1)
    item_lower = (lower_edge + item_shift) ** 2 + item_spread
    item_upper = (upper_edge + item_shift) ** 2 + item_spread
    zero_rim = jnp.zeros((1, width_y, width_z), jnp.float32)

    def grid_shifted(field):
        return (
            diffusion(field, zero_rim, zero_rim, cond_full, zero_rim, zero_rim)
            + (react_full + item_shift) * field
        )

    def grid_system(field):
        return grid_shifted(grid_shifted(field)) + item_spread * field

    solved_grid = chebyshev(grids, grid_system, item_lower, item_upper)
    operator_grid = grid_shifted(solved_grid)
    operator_back, solved_back = (
        lax.all_to_all(operator_grid, "space", split_axis=1, concat_axis=0, tiled=True),
        lax.all_to_all(solved_grid, "space", split_axis=1, concat_axis=0, tiled=True),
    )
    operator_output = operator_back.reshape((2, 2, slot_count, width_x, width_y, width_z))
    solved = solved_back.reshape((2, 2, slot_count, width_x, width_y, width_z))
    twists = twist_slot.reshape(slot_count, 1, 1, 1)
    first_real = solved[0, 0]
    first_imag = solved[0, 1]
    second_real = solved[1, 0]
    second_imag = solved[1, 1]
    twisted = jnp.stack(
        [
            jnp.stack(
                [
                    -twists * first_imag + coupling * second_real,
                    twists * first_real + coupling * second_imag,
                ]
            ),
            jnp.stack([-first_real + twists * second_imag, -first_imag - twists * second_real]),
        ]
    )
    correction = (operator_output - twisted).reshape(2, 2, slot_count, cell_count)
    sampled_entries = jnp.einsum(
        "rkt,mrkc->mtc",
        inverse,
        lax.all_to_all(correction, "tm", split_axis=3, concat_axis=2, tiled=True),
        precision=highest,
    )
    delta_steps = lax.all_to_all(sampled_entries, "tm", split_axis=1, concat_axis=2, tiled=True)
    delta_steps = delta_steps.reshape((2, local_steps, width_x, width_y, width_z))
    return (state_field - delta_steps[0], adjoint - delta_steps[1])


def solution(mesh):
    in_specs = (
        P("tm", "space", None, None),
        P("tm", "space", None, None),
        P("tm", "space", None, None),
        P("space", None, None),
        P("space", None, None),
        P("space", None, None),
    )
    out_specs = (P("tm", "space", None, None), P("tm", "space", None, None))
    return jax.shard_map(shards, mesh=mesh, in_specs=in_specs, out_specs=out_specs, check_vma=False)
```

profile of v0, /device:TPU:1, one launch (start us, length us, event | category | flops | bytes accessed | tf_op | source)
XLA Modules:
  0.0 242.2 jit_solution(7087105304895685468)
XLA Ops:
  2.9 5.1 %collective-permute-start.1 = (f32[5,1,16,128]{3,2,1,0:T(8,128)S(1)}, f32[5,1,16,128]{3,2,1,0:T(8,128)S(1)}, u32[]{:S(2)}, u32[]{:S(2)}) collective-permute-start(f32[5,1,16,128]{3,2,1,0:T(8,128)S(1)} %get-tuple-element.57), channel_id=1, source_target_pairs={{1,0},{2,1},{3,2},{5,4},{6,5},{7,6},{9,8},{10,9},{11,10},{13,12},{... | collective-permute-start | bytes 122888 | tf_op jit(solution)/shard_map/ppermute | solution.py:32
  8.0 7.0 %collective-permute-start.2 = (f32[5,1,16,128]{3,2,1,0:T(8,128)S(1)}, f32[5,1,16,128]{3,2,1,0:T(8,128)S(1)}, u32[]{:S(2)}, u32[]{:S(2)}) collective-permute-start(f32[5,1,16,128]{3,2,1,0:T(8,128)S(1)} %get-tuple-element.56), channel_id=1, source_target_pairs={{0,1},{1,2},{2,3},{4,5},{5,6},{6,7},{8,9},{9,10},{10,11},{12,13},{... | collective-permute-start | bytes 122888 | tf_op jit(solution)/shard_map/ppermute | solution.py:29
  15.8 3.1 %collective-permute-start = (f32[4,16,128]{2,1,0:T(8,128)S(1)}, f32[4,16,128]{2,1,0:T(8,128)S(1)}, u32[]{:S(2)}, u32[]{:S(2)}) collective-permute-start(f32[4,16,128]{2,1,0:T(8,128)S(1)} %get-tuple-element.60), channel_id=1, source_target_pairs={{0,4},{4,8},{8,12},{12,16},{16,20},{20,24},{24,28},{28,32},{32,36}... | collective-permute-start | bytes 98312 | tf_op jit(solution)/shard_map/ppermute | solution.py:21
  19.7 1.3 collective-permute-start.3
  25.3 1.0 subtract_multiply_fusion.2
  30.7 1.0 fusion.118
  31.8 7.9 %copy.39 = f32[2,2,8192]{1,0,2:T(2,128)} copy(f32[2,2,8192]{2,1,0:T(2,128)S(1)} %pad_maximum_fusion) | data formatting | bytes 262144 | tf_op jit(solution)/shard_map/stack | solution.py:181
  39.7 14.0 %reshape.650 = f32[64,1,512]{2,1,0:T(1,128)} reshape(f32[8192,2,2]{2,1,0:T(2,128)} %bitcast.324) | data formatting | bytes 262144
  53.7 10.0 %all-to-all-start = ((f32[64,1,512]{2,1,0:T(1,128)}), f32[64,1,512]{2,1,0:T(1,128)S(1)}, u32[]{:S(2)}, u32[]{:S(2)}) async-start(f32[64,1,512]{2,1,0:T(1,128)} %reshape.650), calls=%async_computation | async-start | bytes 262144 | tf_op jit(solution)/shard_map/all_to_all | solution.py:210
  63.9 9.5 %all-to-all-done = f32[64,1,512]{2,1,0:T(1,128)S(1)} async-done(((f32[64,1,512]{2,1,0:T(1,128)}), f32[64,1,512]{2,1,0:T(1,128)S(1)}, u32[]{:S(2)}, u32[]{:S(2)}) %all-to-all-start) | async-done | bytes 131104 | tf_op jit(solution)/shard_map/all_to_all | solution.py:210
  75.0 14.3 %reshape.651 = f32[8192,2,2]{2,1,0:T(2,128)} reshape(f32[64,512]{1,0:T(8,128)S(1)} %reduce) | data formatting | bytes 262144
  89.2 9.3 %copy.40 = f32[2,2,64,128]{3,1,2,0:T(2,128)S(1)} copy(f32[2,2,64,128]{1,0,3,2:T(2,128)} %bitcast.325) | data formatting | bytes 262144 | tf_op jit(solution)/shard_map/all_to_all | solution.py:210
  99.6 4.6 %all-to-all-start.1 = ((f32[2,2,64,128]{3,1,0,2:T(2,128)}), f32[2,2,64,128]{3,1,0,2:T(2,128)S(1)}, u32[]{:S(2)}, u32[]{:S(2)}) async-start(f32[2,2,64,128]{3,1,0,2:T(2,128)} %copy.41), calls=%async_computation.1 | async-start | bytes 262144 | tf_op jit(solution)/shard_map/all_to_all | solution.py:213
  105.1 8.8 %all-to-all-done.1 = f32[2,2,64,128]{3,1,0,2:T(2,128)S(1)} async-done(((f32[2,2,64,128]{3,1,0,2:T(2,128)}), f32[2,2,64,128]{3,1,0,2:T(2,128)S(1)}, u32[]{:S(2)}, u32[]{:S(2)}) %all-to-all-start.1) | async-done | bytes 131104 | tf_op jit(solution)/shard_map/all_to_all | solution.py:213
  114.5 4.8 %all-to-all-start.2 = ((f32[4,4,16,128]{3,2,1,0:T(8,128)}), f32[4,4,16,128]{3,2,1,0:T(8,128)S(1)}, u32[]{:S(2)}, u32[]{:S(2)}) async-start(f32[4,4,16,128]{3,2,1,0:T(8,128)} %copy.42), calls=%async_computation.2 | async-start | bytes 262144 | tf_op jit(solution)/shard_map/all_to_all | solution.py:218
  119.4 10.7 %all_gather.3 = f32[16,32,128]{2,1,0:T(8,128)S(1)} all-gather(f32[4,32,128]{2,1,0:T(8,128)S(1)} %pad_maximum_fusion.2), channel_id=1, replica_groups=mesh['tm'=64,'space'=4] {'space'}, dimensions={0}, use_global_device_ids=true | all-gather | bytes 327680 | tf_op jit(solution)/shard_map/all_gather | solution.py:39
  135.2 1.0 fusion.1
  136.2 1.1 fusion
  137.3 1.0 fusion.96
  139.1 6.4 %all-to-all-start.4 = ((f32[1,16,16,128]{3,2,0,1:T(8,128)}), f32[1,16,16,128]{3,2,0,1:T(8,128)S(1)}, u32[]{:S(2)}, u32[]{:S(2)}) async-start(f32[1,16,16,128]{3,2,0,1:T(8,128)} %bitcast.52), calls=%async_computation.4 | async-start | bytes 262144 | tf_op jit(solution)/shard_map/all_to_all | solution.py:248
  145.4 1.7 fusion.81
  147.2 5.8 %all-to-all-done.4 = f32[1,16,16,128]{3,2,0,1:T(8,128)S(1)} async-done(((f32[1,16,16,128]{3,2,0,1:T(8,128)}), f32[1,16,16,128]{3,2,0,1:T(8,128)S(1)}, u32[]{:S(2)}, u32[]{:S(2)}) %all-to-all-start.4) | async-done | bytes 131104 | tf_op jit(solution)/shard_map/all_to_all | solution.py:248
  152.9 4.3 %all-to-all-start.3 = ((f32[1,16,16,128]{3,2,0,1:T(8,128)}), f32[1,16,16,128]{3,2,0,1:T(8,128)S(1)}, u32[]{:S(2)}, u32[]{:S(2)}) async-start(f32[1,16,16,128]{3,2,0,1:T(8,128)} %fusion.81), calls=%async_computation.3 | async-start | bytes 262144 | tf_op jit(solution)/shard_map/all_to_all | solution.py:247
  157.3 7.5 %all-to-all-done.3 = f32[1,16,16,128]{3,2,0,1:T(8,128)S(1)} async-done(((f32[1,16,16,128]{3,2,0,1:T(8,128)}), f32[1,16,16,128]{3,2,0,1:T(8,128)S(1)}, u32[]{:S(2)}, u32[]{:S(2)}) %all-to-all-start.3) | async-done | bytes 131104 | tf_op jit(solution)/shard_map/all_to_all | solution.py:247
  164.9 7.8 %copy.45 = f32[2,2,1,8192]{1,0,2,3:T(2,128)} copy(f32[2,2,1,8192]{3,2,1,0:T(1,128)S(1)} %maximum_subtract_fusion) | data formatting | bytes 262144 | tf_op jit(solution)/shard_map/sub | solution.py:268
  172.7 14.0 %reshape.652 = f32[64,1,512]{2,1,0:T(1,128)} reshape(f32[8192,1,2,2]{3,2,1,0:T(2,128)} %bitcast.326) | data formatting | bytes 262144
  186.7 8.3 %all-to-all-start.5 = ((f32[64,1,512]{2,1,0:T(1,128)}), f32[64,1,512]{2,1,0:T(1,128)S(1)}, u32[]{:S(2)}, u32[]{:S(2)}) async-start(f32[64,1,512]{2,1,0:T(1,128)} %reshape.652), calls=%async_computation.5 | async-start | bytes 262144 | tf_op jit(solution)/shard_map/all_to_all | solution.py:272
  195.2 9.5 %all-to-all-done.5 = f32[64,1,512]{2,1,0:T(1,128)S(1)} async-done(((f32[64,1,512]{2,1,0:T(1,128)}), f32[64,1,512]{2,1,0:T(1,128)S(1)}, u32[]{:S(2)}, u32[]{:S(2)}) %all-to-all-start.5) | async-done | bytes 131104 | tf_op jit(solution)/shard_map/all_to_all | solution.py:272
  204.7 1.0 reduce.1
  205.7 14.3 %reshape.653 = f32[8192,1,2,2]{3,2,1,0:T(2,128)} reshape(f32[64,512]{1,0:T(8,128)S(1)} %reduce.1) | data formatting | bytes 262144
  220.0 6.8 %copy.53 = f32[2,2,64,128]{3,2,1,0:T(8,128)S(1)} copy(f32[2,2,64,128]{1,0,3,2:T(2,128)} %bitcast.327) | data formatting | bytes 262144 | tf_op jit(solution)/shard_map/all_to_all | solution.py:272
  227.3 13.6 %all_to_all.84 = f32[2,128,128]{2,0,1:T(2,128)S(1)} all-to-all(f32[2,128,128]{2,0,1:T(2,128)S(1)} %copy.47), channel_id=1, replica_groups=mesh['tm'=64,'space'=4] {'tm'}, dimensions={1} | all-to-all | bytes 262144 | tf_op jit(solution)/shard_map/all_to_all | solution.py:275
  (129 shorter events, 23.6 us)
Async XLA Ops:
  2.9 25.3 %collective-permute-start.1 = (f32[5,1,16,128]{3,2,1,0:T(8,128)S(1)}, f32[5,1,16,128]{3,2,1,0:T(8,128)S(1)}, u32[]{:S(2)}, u32[]{:S(2)}) collective-permute-start(f32[5,1,16,128]{3,2,1,0:T(8,128)S(1)} %get-tuple-element.57), channel_id=1, source_target_pairs={{1,0},{2,1},{3,2},{5,4},{6,5},{7,6},{9,8},{10,9},{11,10},{13,12},{... | collective-permute-start | bytes 122888 | tf_op jit(solution)/shard_map/ppermute | solution.py:32
  8.0 20.2 %collective-permute-start.2 = (f32[5,1,16,128]{3,2,1,0:T(8,128)S(1)}, f32[5,1,16,128]{3,2,1,0:T(8,128)S(1)}, u32[]{:S(2)}, u32[]{:S(2)}) collective-permute-start(f32[5,1,16,128]{3,2,1,0:T(8,128)S(1)} %get-tuple-element.56), channel_id=1, source_target_pairs={{0,1},{1,2},{2,3},{4,5},{5,6},{6,7},{8,9},{9,10},{10,11},{12,13},{... | collective-permute-start | bytes 122888 | tf_op jit(solution)/shard_map/ppermute | solution.py:29
  15.8 11.6 %collective-permute-start = (f32[4,16,128]{2,1,0:T(8,128)S(1)}, f32[4,16,128]{2,1,0:T(8,128)S(1)}, u32[]{:S(2)}, u32[]{:S(2)}) collective-permute-start(f32[4,16,128]{2,1,0:T(8,128)S(1)} %get-tuple-element.60), channel_id=1, source_target_pairs={{0,4},{4,8},{8,12},{12,16},{16,20},{20,24},{24,28},{28,32},{32,36}... | collective-permute-start | bytes 98312 | tf_op jit(solution)/shard_map/ppermute | solution.py:21
  19.7 11.0 %collective-permute-start.3 = (f32[4,16,128]{2,1,0:T(8,128)S(1)}, f32[4,16,128]{2,1,0:T(8,128)S(1)}, u32[]{:S(2)}, u32[]{:S(2)}) collective-permute-start(f32[4,16,128]{2,1,0:T(8,128)S(1)} %get-tuple-element.71), channel_id=1, source_target_pairs={{4,0},{8,4},{12,8},{16,12},{20,16},{24,20},{28,24},{32,28},{36,32}... | collective-permute-start | bytes 98312 | tf_op jit(solution)/shard_map/ppermute | solution.py:21
  53.7 19.7 %all-to-all-start = ((f32[64,1,512]{2,1,0:T(1,128)}), f32[64,1,512]{2,1,0:T(1,128)S(1)}, u32[]{:S(2)}, u32[]{:S(2)}) async-start(f32[64,1,512]{2,1,0:T(1,128)} %reshape.650), calls=%async_computation | async-start | bytes 262144 | tf_op jit(solution)/shard_map/all_to_all | solution.py:210
  74.9 44.4 %copy-start.2 = (f32[4,16,128]{2,1,0:T(8,128)S(1)}, f32[4,16,128]{2,1,0:T(8,128)}, u32[]{:S(2)}) copy-start(f32[4,16,128]{2,1,0:T(8,128)} %param.10) | copy-start | bytes 98308
  75.0 44.4 %copy-start.3 = (f32[4,16,128]{2,1,0:T(8,128)S(1)}, f32[4,16,128]{2,1,0:T(8,128)}, u32[]{:S(2)}) copy-start(f32[4,16,128]{2,1,0:T(8,128)} %param.11) | copy-start | bytes 98308
  99.6 14.3 %all-to-all-start.1 = ((f32[2,2,64,128]{3,1,0,2:T(2,128)}), f32[2,2,64,128]{3,1,0,2:T(2,128)S(1)}, u32[]{:S(2)}, u32[]{:S(2)}) async-start(f32[2,2,64,128]{3,1,0,2:T(2,128)} %copy.41), calls=%async_computation.1 | async-start | bytes 262144 | tf_op jit(solution)/shard_map/all_to_all | solution.py:213
  114.5 15.5 %all-to-all-start.2 = ((f32[4,4,16,128]{3,2,1,0:T(8,128)}), f32[4,4,16,128]{3,2,1,0:T(8,128)S(1)}, u32[]{:S(2)}, u32[]{:S(2)}) async-start(f32[4,4,16,128]{3,2,1,0:T(8,128)} %copy.42), calls=%async_computation.2 | async-start | bytes 262144 | tf_op jit(solution)/shard_map/all_to_all | solution.py:218
  139.1 13.9 %all-to-all-start.4 = ((f32[1,16,16,128]{3,2,0,1:T(8,128)}), f32[1,16,16,128]{3,2,0,1:T(8,128)S(1)}, u32[]{:S(2)}, u32[]{:S(2)}) async-start(f32[1,16,16,128]{3,2,0,1:T(8,128)} %bitcast.52), calls=%async_computation.4 | async-start | bytes 262144 | tf_op jit(solution)/shard_map/all_to_all | solution.py:248
  152.9 11.8 %all-to-all-start.3 = ((f32[1,16,16,128]{3,2,0,1:T(8,128)}), f32[1,16,16,128]{3,2,0,1:T(8,128)S(1)}, u32[]{:S(2)}, u32[]{:S(2)}) async-start(f32[1,16,16,128]{3,2,0,1:T(8,128)} %fusion.81), calls=%async_computation.3 | async-start | bytes 262144 | tf_op jit(solution)/shard_map/all_to_all | solution.py:247
  186.7 18.0 %all-to-all-start.5 = ((f32[64,1,512]{2,1,0:T(1,128)}), f32[64,1,512]{2,1,0:T(1,128)S(1)}, u32[]{:S(2)}, u32[]{:S(2)}) async-start(f32[64,1,512]{2,1,0:T(1,128)} %reshape.652), calls=%async_computation.5 | async-start | bytes 262144 | tf_op jit(solution)/shard_map/all_to_all | solution.py:272
  205.7 35.2 %copy-start = (f32[2,4,16,128]{3,2,1,0:T(8,128)S(1)}, f32[2,4,16,128]{3,2,1,0:T(8,128)}, u32[]{:S(2)}) copy-start(f32[2,4,16,128]{3,2,1,0:T(8,128)} %param.7) | copy-start | bytes 196612
  205.7 35.9 %copy-start.1 = (f32[2,4,16,128]{3,2,1,0:T(8,128)S(1)}, f32[2,4,16,128]{3,2,1,0:T(8,128)}, u32[]{:S(2)}) copy-start(f32[2,4,16,128]{3,2,1,0:T(8,128)} %param.6) | copy-start | bytes 196612
where the time goes:
time: 245 us; the launch traced here: 242 us
  local copies, waits for them, and re-layouts  94.3 us (38%)
  starting transfers between devices  55 us (22%)
  waiting for transfers between devices  41.1 us (17%)
  other arithmetic  24.7 us (10%)
  blocking collectives  24.3 us (10%)
    unnamed x12, local copies, waits for them, and re-layouts  56.5 us
    all_to_all x1, blocking collectives, shards(): lax.all_to_all(sampled_entries, 'tm', split_axis=1, concat_axis=2, tiled=...  13.6 us
    all_gather x1, blocking collectives, in_one_piece(): lax.all_gather(both, axis, axis=dim, tiled=True)  10.7 us
    all_to_all x1, starting transfers between devices, shards(): lax.all_to_all(residual, 'tm', split_axis=2, concat_axis=1, tiled=True)  10 us
    all_to_all x2, local copies, waits for them, and re-layouts, shards(): lax.all_to_all(residual, 'tm', split_axis=2, concat_axis=1, tiled=True)  9.89 us
    all_to_all x1, waiting for transfers between devices, shards(): lax.all_to_all(correction, 'tm', split_axis=3, concat_axis=2, tiled=True)  9.51 us
    all_to_all x1, waiting for transfers between devices, shards(): lax.all_to_all(residual, 'tm', split_axis=2, concat_axis=1, tiled=True)  9.5 us
    all_to_all x1, waiting for transfers between devices, shards(): lax.all_to_all(spectral, 'tm', split_axis=2, concat_axis=3, tiled=True)  8.81 us
  transfers between devices with their start and end apart: 10, of which 5 were waited for; matrix products, arithmetic and copies ran while one was open for 5% of the time, Pallas kernels for 0%

commit v1 on v0

v1 whole, which is shorter than its diff:
```python
import functools

import jax
import jax.numpy as jnp
import numpy as np
from jax import lax
from jax.experimental import pallas as pl
from jax.experimental.pallas import tpu as pltpu
from jax.sharding import PartitionSpec as P

CHEB = 8
step_rate = 2.0
coupling = 1.0
lower_edge = 0.05
upper_edge = 7.0
COEF = 32
vmem = functools.partial(pl.BlockSpec, memory_space=pltpu.VMEM)
grant = pltpu.CompilerParams(vmem_limit_bytes=8 * 1024 * 1024)
smem = functools.partial(pl.BlockSpec, memory_space=pltpu.SMEM)


def time_tables(horizon, slots):
    k = np.arange(slots)[:, None]
    n = np.concatenate([np.arange(0, horizon, 2), np.arange(1, horizon, 2)])[None, :]
    angle = 2.0 * np.pi / horizon * ((k * n) % horizon)
    cosine, sine = np.cos(angle), np.sin(angle)
    alternation = np.where(n % 2 == 0, 1.0, -1.0)
    forward = np.concatenate([cosine, np.where(k == 0, alternation, -sine)], 0)
    inverse = (
        np.concatenate(
            [
                np.where(k == 0, 1.0, 2.0) * cosine,
                np.where(k == 0, alternation, -2.0 * sine),
            ],
            0,
        )
        / horizon
    )
    return forward.astype(np.float32), inverse.T.astype(np.float32)


def solver_table(horizon, slots):
    theta = 2.0 * np.pi / horizon * np.arange(slots + 1)
    shift = step_rate * (1.0 - np.cos(theta))
    twist = step_rate * np.sin(theta)
    twist[slots] = 0.0
    spread = twist * twist + coupling
    lower = (lower_edge + shift) ** 2 + spread
    upper = (upper_edge + shift) ** 2 + spread
    centre = 0.5 * (upper + lower)
    half = 0.5 * (upper - lower)
    ratio = centre / half
    rho = 1.0 / ratio
    table = np.zeros((slots + 1, COEF))
    table[:, 0] = shift
    table[:, 1] = spread
    table[:, 2] = 1.0 / centre
    for step in range(CHEB - 1):
        rho_next = 1.0 / (2.0 * ratio - rho)
        table[:, 4 + 2 * step] = rho_next * rho
        table[:, 5 + 2 * step] = 2.0 * rho_next / half
        rho = rho_next
    return table.reshape(-1).astype(np.float32), twist[:slots]


def pack_kernel(y_ref, p_ref, t_ref, c_ref, r_ref, o_ref, m_ref):
    m_ref[0] = c_ref[...]
    m_ref[1] = r_ref[...]
    for j in range(2):
        y = y_ref[j]
        p = p_ref[j]
        square = y * y
        o_ref[:, j, :] = y
        o_ref[:, 2 + j, :] = p
        o_ref[:, 4 + j, :] = square * y * (1.0 / 3.0) + coupling * p
        o_ref[:, 6 + j, :] = square * p - y + t_ref[j]


def forward_kernel(f_ref, init_ref, x_ref, o_ref):
    rows = x_ref.shape[0]
    lanes = x_ref.shape[2]
    mine = lax.axis_index("tm")
    y0, y1, p0, p1, g0, g1, h0, h1 = (x_ref[:, i, :] for i in range(8))
    row = lax.broadcasted_iota(jnp.int32, (rows, lanes), 0)
    before = jnp.where(row == 0, init_ref[pl.ds(mine, 1), :], pltpu.roll(y1, 1, 0))
    after = jnp.where(row == rows - 1, 0.0, pltpu.roll(p0, rows - 1, 0))
    a0 = g0 + step_rate * (y0 - before)
    a1 = g1 + step_rate * (y1 - y0)
    b0 = h0 + step_rate * (p0 - p1)
    b1 = h1 + step_rate * (p1 - after)
    data = jnp.concatenate(
        [
            jnp.concatenate([a0, b0, y0, p0], 1),
            jnp.concatenate([a1, b1, y1, p1], 1),
        ],
        0,
    )
    hat = lax.dot(
        f_ref[...], data, precision=lax.Precision.HIGHEST, preferred_element_type=jnp.float32
    )
    for f in range(2):
        for r in range(2):
            for q in range(2):
                column = (q * 2 + f) * lanes
                o_ref[:, (f * 2 + r) * 2 + q, :] = hat[
                    r * rows : (r + 1) * rows, column : column + lanes
                ]


def solve_kernel(
    co_ref,
    m0_ref,
    m1_ref,
    m2_ref,
    m3_ref,
    x_ref,
    o_ref,
    mat,
    cx,
    cyp,
    cym,
    czp,
    czm,
    diag,
    yy,
    res,
    d,
    t,
    w,
):
    slot = lax.axis_index("tm")
    item = lax.axis_index("space")
    slots = x_ref.shape[0]
    frequency = jnp.where((slot == 0) & (item % 2 == 1), slots, slot)
    base = frequency * COEF
    shift = co_ref[base]
    spread = co_ref[base + 1]
    start = co_ref[base + 2]
    for piece, ref in enumerate((m0_ref, m1_ref, m2_ref, m3_ref)):
        mat[item ^ piece] = ref[...]
    slabs = 4
    width = mat.shape[2]
    count_y, lanes = mat.shape[3], mat.shape[4]
    count = slabs * width
    row = lax.broadcasted_iota(jnp.int32, (count_y, lanes), 0)
    lane = lax.broadcasted_iota(jnp.int32, (count_y, lanes), 1)

    def cond(x):
        return mat[x // width, 0, x % width]

    for x in range(count):
        c = cond(x)
        half = 0.5 * c
        total = mat[x // width, 1, x % width] + shift
        up = 0.5 * (c + cond(x + 1)) if x + 1 < count else half
        down = 0.5 * (c + cond(x - 1)) if x > 0 else half
        if x + 1 < count:
            cx[x] = up
        yp = jnp.where(row == count_y - 1, 0.0, 0.5 * pltpu.roll(c, count_y - 1, 0)) + half
        ym = jnp.where(row == 0, 0.0, 0.5 * pltpu.roll(c, 1, 0)) + half
        zp = jnp.where(lane == lanes - 1, 0.0, 0.5 * pltpu.roll(c, lanes - 1, 1)) + half
        zm = jnp.where(lane == 0, 0.0, 0.5 * pltpu.roll(c, 1, 1)) + half
        diag[x] = (up + down) + (yp + ym) + (zp + zm) + total
        cyp[x] = jnp.where(row == count_y - 1, 0.0, yp)
        cym[x] = jnp.where(row == 0, 0.0, ym)
        czp[x] = jnp.where(lane == lanes - 1, 0.0, zp)
        czm[x] = jnp.where(lane == 0, 0.0, zm)
    for s in range(slabs):
        res[s * width : (s + 1) * width] = x_ref[:, 2 * s, :].reshape(width, count_y, lanes)
        yy[s * width : (s + 1) * width] = x_ref[:, 2 * s + 1, :].reshape(width, count_y, lanes)

    def applied(ref, x):
        v = ref[x]
        out = diag[x] * v
        if x + 1 < count:
            out = out - cx[x] * ref[x + 1]
        if x > 0:
            out = out - cx[x - 1] * ref[x - 1]
        out = out - cyp[x] * pltpu.roll(v, count_y - 1, 0)
        out = out - cym[x] * pltpu.roll(v, 1, 0)
        out = out - czp[x] * pltpu.roll(v, lanes - 1, 1)
        out = out - czm[x] * pltpu.roll(v, 1, 1)
        return v, out

    for x in range(count):
        v, out = applied(yy, x)
        r = res[x] + out - (mat[x // width, 1, x % width] + shift) * v
        first = start * r
        res[x] = r
        d[x] = first
        w[x] = first

    def step(i, carry):
        alpha = co_ref[base + 4 + 2 * i]
        beta = co_ref[base + 5 + 2 * i]
        for x in range(count):
            t[x] = applied(d, x)[1]
        for x in range(count):
            now = d[x]
            r = res[x] - (applied(t, x)[1] + spread * now)
            now = alpha * now + beta * r
            res[x] = r
            d[x] = now
            w[x] = w[x] + now
        return carry

    lax.fori_loop(0, CHEB - 1, step, 0)
    for x in range(count):
        t[x] = applied(w, x)[1]
    for s in range(slabs):
        o_ref[:, 2 * s, :] = w[s * width : (s + 1) * width].reshape(width * count_y, lanes)
        o_ref[:, 2 * s + 1, :] = t[s * width : (s + 1) * width].reshape(width * count_y, lanes)


def inverse_kernel(g_ref, b_ref, x_ref, o_ref):
    rows = x_ref.shape[0]
    lanes = x_ref.shape[2]
    b = b_ref[...]
    u_re, ku_re, u_im, ku_im, v_re, kv_re, v_im, kv_im = (x_ref[:, i, :] for i in range(8))
    c00 = ku_re - (coupling * v_re - b * u_im)
    c01 = ku_im - (coupling * v_im + b * u_re)
    c10 = kv_re - (b * v_im - u_re)
    c11 = kv_im + (b * v_re + u_im)
    data = jnp.concatenate(
        [jnp.concatenate([c00, c10], 1), jnp.concatenate([c01, c11], 1)],
        0,
    )
    back = lax.dot(
        g_ref[...], data, precision=lax.Precision.HIGHEST, preferred_element_type=jnp.float32
    )
    for f in range(2):
        for j in range(2):
            o_ref[:, f * 2 + j, :] = back[
                j * rows : (j + 1) * rows, f * lanes : (f + 1) * lanes
            ]


def update_kernel(y_ref, p_ref, d_ref, ny_ref, np_ref):
    for j in range(2):
        ny_ref[j] = y_ref[j] - d_ref[:, j, :]
        np_ref[j] = p_ref[j] - d_ref[:, 2 + j, :]


def swapped(value, distance):
    count = lax.axis_size("space")
    return lax.ppermute(value, "space", [(i, i ^ distance) for i in range(count)])


def shards(state_field, adjoint, target, initial_state, conductivity, reaction):
    steps, width_x, width_y, width_z = state_field.shape
    devices = lax.axis_size("tm")
    spaces = lax.axis_size("space")
    rows = width_x * width_y
    horizon = steps * devices
    assert steps == 2 and rows == devices and spaces == 4
    f32 = jnp.float32

    def shape(*dims):
        return jax.ShapeDtypeStruct(dims, f32)

    flat = (steps, rows, width_z)
    state_rows = state_field.reshape(flat)
    adjoint_rows = adjoint.reshape(flat)
    packed, material = pl.pallas_call(
        pack_kernel,
        out_shape=(
            shape(rows, 8, width_z),
            shape(2, width_x, width_y, width_z),
        ),
        in_specs=[vmem()] * 5,
        out_specs=(vmem(), vmem()),
        compiler_params=grant,
        name="pack",
    )(state_rows, adjoint_rows, target.reshape(flat), conductivity, reaction)
    material_core = swapped(material, 1)
    material_far = swapped(material, 2)
    material_both = swapped(material, 3)
    forward, inverse = time_tables(horizon, devices)
    table, twist = solver_table(horizon, devices)
    by_cell = lax.all_to_all(packed, "tm", 0, 0, tiled=True)
    hat = pl.pallas_call(
        forward_kernel,
        out_shape=shape(devices, 8, width_z),
        in_specs=[vmem()] * 3,
        out_specs=vmem(),
        compiler_params=grant,
        name="forward",
    )(jnp.asarray(forward), initial_state.reshape(rows, width_z), by_cell)
    everyone = ("tm", "space")
    pairs = (devices * spaces, 2, width_z)
    by_item = lax.all_to_all(hat.reshape(pairs), everyone, 0, 0, tiled=True)
    grid = (spaces * width_x, width_y, width_z)
    solved = pl.pallas_call(
        solve_kernel,
        out_shape=shape(rows, 8, width_z),
        in_specs=[smem()] + [vmem()] * 5,
        out_specs=vmem(),
        scratch_shapes=[pltpu.VMEM((spaces, 2, width_x, width_y, width_z), f32)]
        + [pltpu.VMEM(grid, f32)] * 11,
        compiler_params=grant,
        name="solve",
    )(
        jnp.asarray(table),
        material,
        material_core,
        material_far,
        material_both,
        by_item.reshape(rows, 8, width_z),
    )
    by_row = lax.all_to_all(solved.reshape(pairs), everyone, 0, 0, tiled=True)
    twists = np.broadcast_to(twist.astype(np.float32)[:, None], (devices, width_z))
    delta = pl.pallas_call(
        inverse_kernel,
        out_shape=shape(devices, 4, width_z),
        in_specs=[vmem()] * 3,
        out_specs=vmem(),
        compiler_params=grant,
        name="inverse",
    )(jnp.asarray(inverse), jnp.asarray(twists), by_row.reshape(devices, 8, width_z))
    by_time = lax.all_to_all(delta, "tm", 0, 0, tiled=True)
    new_state, new_adjoint = pl.pallas_call(
        update_kernel,
        out_shape=(shape(*flat), shape(*flat)),
        in_specs=[vmem()] * 3,
        out_specs=(vmem(), vmem()),
        compiler_params=grant,
        name="update",
    )(state_rows, adjoint_rows, by_time)
    return new_state.reshape(state_field.shape), new_adjoint.reshape(adjoint.shape)


def solution(mesh):
    in_specs = (
        P("tm", "space", None, None),
        P("tm", "space", None, None),
        P("tm", "space", None, None),
        P("space", None, None),
        P("space", None, None),
        P("space", None, None),
    )
    out_specs = (P("tm", "space", None, None), P("tm", "space", None, None))
    return jax.shard_map(shards, mesh=mesh, in_specs=in_specs, out_specs=out_specs, check_vma=False)
```

time: 245 us -> 102 us (0.42)
  local copies, waits for them, and re-layouts: 94.3 us -> 4.79 us
  blocking collectives: 24.3 us -> 63.5 us
  starting transfers between devices: 55 us -> 18 us
  waiting for transfers between devices: 41.1 us -> 8.7 us
  other arithmetic: 24.7 us -> 0 us
  Pallas kernels: 0 us -> 5.73 us
    unnamed x12 -> x24, local copies, waits for them, and re-layouts: 56.5 us -> 4.72 us
    all_to_all x1 -> x3, blocking collectives: 13.6 us -> 63.5 us  [the longest x1 25.7 us: shards(): by_row = lax.all_to_all(solved.reshape(pairs), everyone, 0, 0, tiled=True)]
    all_to_all x6 -> x1, waiting for transfers between devices: 41 us -> 0.01 us  [shards(): by_item = lax.all_to_all(hat.reshape(pairs), everyone, 0, 0, tiled=True)]
    all_to_all x6 -> x1, starting transfers between devices: 38.5 us -> 10.1 us  [shards(): by_item = lax.all_to_all(hat.reshape(pairs), everyone, 0, 0, tiled=True)]
    all_to_all x4 -> x0, local copies, waits for them, and re-layouts: 16.7 us -> none  [the longest x2 9.89 us: shards(): lax.all_to_all(residual, 'tm', split_axis=2, concat_axis=1, tiled=True)]
    mul x71 -> x0, other arithmetic: 13.9 us -> none  [the longest x32 5.88 us: face_term(): face_cond * (lax.slice_in_dim(values, 0, length - 1, axis=value_axis) - l...]
    all_gather x1 -> x0, blocking collectives: 10.7 us -> none  [in_one_piece(): lax.all_gather(both, axis, axis=dim, tiled=True)]
    ppermute x4 -> x3, waiting for transfers between devices: 0.01 us -> 8.7 us  [swapped(): lax.ppermute(value, 'space', [(i, i ^ distance) for i in range(count)])]
  transfers between devices with their start and end apart: 10 -> 4, of which waited for: 5 -> 2; matrix products, arithmetic and copies ran while one was open for 5% -> 0% of each run, Pallas kernels for 0% -> 0%
where the time goes in v1:
time: 102 us; the launch traced here: 101 us
  blocking collectives  63.5 us (62%)
  starting transfers between devices  18 us (18%)
  waiting for transfers between devices  8.7 us (9%)
  Pallas kernels  5.73 us (6%)
  local copies, waits for them, and re-layouts  4.79 us (5%)
    all_to_all x1, blocking collectives, shards(): by_row = lax.all_to_all(solved.reshape(pairs), everyone, 0, 0, tiled=True)  25.7 us
    all_to_all x1, blocking collectives, shards(): by_cell = lax.all_to_all(packed, 'tm', 0, 0, tiled=True)  23.7 us
    all_to_all x1, blocking collectives, shards(): by_time = lax.all_to_all(delta, 'tm', 0, 0, tiled=True)  14.1 us
    all_to_all x1, starting transfers between devices, shards(): by_item = lax.all_to_all(hat.reshape(pairs), everyone, 0, 0, tiled=True)  10.1 us
    ppermute x3, waiting for transfers between devices, swapped(): lax.ppermute(value, 'space', [(i, i ^ distance) for i in range(count)])  8.7 us
    ppermute x3, starting transfers between devices, swapped(): lax.ppermute(value, 'space', [(i, i ^ distance) for i in range(count)])  7.87 us
    unnamed x24, local copies, waits for them, and re-layouts  4.72 us
    pallas_call x1, Pallas kernels, shards(): pl.pallas_call(solve_kernel, out_shape=shape(rows, 8, width_z), in_specs=...  3.03 us
  transfers between devices with their start and end apart: 4, of which 2 were waited for; matrix products, arithmetic and copies ran while one was open for 0% of the time, Pallas kernels for 0%

profile of v1, /device:TPU:1, one launch (start us, length us, event | category | flops | bytes accessed | tf_op | source)
XLA Modules:
  0.0 101.4 jit_solution(9761207815172812106)
XLA Ops:
  0.6 0.0 copy-start
  0.6 0.8 copy-done
  1.5 0.8 copy-done.2
  2.3 0.8 copy-done.6
  3.2 0.8 copy-done.8
  3.9 0.8 copy-done.9
  4.7 0.2 pack.1
  4.8 0.0 copy-start.5
  4.8 0.0 copy-start.7
  4.9 23.7 %all_to_all.20.x_ref = f32[64,8,128]{2,1,0:T(8,128)S(1)} all-to-all(f32[64,8,128]{2,1,0:T(8,128)S(1)} %get-tuple-element.7), channel_id=1, replica_groups=mesh['tm'=64,'space'=4] {'tm'}, dimensions={0} | all-to-all | bytes 524288 | tf_op jit(solution)/shard_map/all_to_all | solution.py:280
  28.6 0.0 copy-done.5
  28.6 0.0 copy-done.7
  28.6 1.4 %forward.1 = f32[64,8,128]{2,1,0:T(8,128)} custom-call(f32[128,128]{1,0:T(8,128)S(1)} %copy-done.5, f32[64,128]{1,0:T(8,128)S(1)} %bitcast.18, f32[64,8,128]{2,1,0:T(8,128)S(1)} %all_to_all.20.x_ref), custom_call_target="tpu_custom_call" | custom-call | tf_op jit(solution)/shard_map/forward/pallas_call | solution.py:281
  29.9 10.1 %all-to-all-start.1 = ((f32[256,2,128]{2,1,0:T(2,128)}), f32[256,2,128]{2,1,0:T(2,128)S(1)}, u32[]{:S(2)}, u32[]{:S(2)}) async-start(f32[256,2,128]{2,1,0:T(2,128)} %bitcast.4), calls=%async_computation.1 | async-start | bytes 524288 | tf_op jit(solution)/shard_map/all_to_all | solution.py:291
  40.1 2.2 %collective-permute-start = (f32[2,4,16,128]{3,2,1,0:T(8,128)S(1)}, f32[2,4,16,128]{3,2,1,0:T(8,128)S(1)}, u32[]{:S(2)}, u32[]{:S(2)}) collective-permute-start(f32[2,4,16,128]{3,2,1,0:T(8,128)S(1)} %get-tuple-element.6.m0_ref), channel_id=1, source_target_pairs={{0,1},{1,0},{2,3},{3,2},{4,5},{5,4},{6,7},{7,6},{8,9},{9,8},{10,11... | collective-permute-start | bytes 196616 | tf_op jit(solution)/shard_map/ppermute | solution.py:246
  42.3 4.4 %collective-permute-start.1 = (f32[2,4,16,128]{3,2,1,0:T(8,128)S(1)}, f32[2,4,16,128]{3,2,1,0:T(8,128)S(1)}, u32[]{:S(2)}, u32[]{:S(2)}) collective-permute-start(f32[2,4,16,128]{3,2,1,0:T(8,128)S(1)} %get-tuple-element.6.m0_ref), channel_id=1, source_target_pairs={{0,2},{1,3},{2,0},{3,1},{4,6},{5,7},{6,4},{7,5},{8,10},{9,11},{10,... | collective-permute-start | bytes 196616 | tf_op jit(solution)/shard_map/ppermute | solution.py:246
  46.8 1.2 %collective-permute-start.2 = (f32[2,4,16,128]{3,2,1,0:T(8,128)S(1)}, f32[2,4,16,128]{3,2,1,0:T(8,128)S(1)}, u32[]{:S(2)}, u32[]{:S(2)}) collective-permute-start(f32[2,4,16,128]{3,2,1,0:T(8,128)S(1)} %get-tuple-element.6.m0_ref), channel_id=1, source_target_pairs={{0,3},{1,2},{2,1},{3,0},{4,7},{5,6},{6,5},{7,4},{8,11},{9,10},{10,... | collective-permute-start | bytes 196616 | tf_op jit(solution)/shard_map/ppermute | solution.py:246
  48.0 0.0 collective-permute-done.m1_ref
  48.0 6.2 %collective-permute-done.1.m2_ref = f32[2,4,16,128]{3,2,1,0:T(8,128)S(1)} collective-permute-done((f32[2,4,16,128]{3,2,1,0:T(8,128)S(1)}, f32[2,4,16,128]{3,2,1,0:T(8,128)S(1)}, u32[]{:S(2)}, u32[]{:S(2)}) %collective-permute-start.1) | collective-permute-done | bytes 65568 | tf_op jit(solution)/shard_map/ppermute | solution.py:246
  54.2 2.5 %collective-permute-done.2.m3_ref = f32[2,4,16,128]{3,2,1,0:T(8,128)S(1)} collective-permute-done((f32[2,4,16,128]{3,2,1,0:T(8,128)S(1)}, f32[2,4,16,128]{3,2,1,0:T(8,128)S(1)}, u32[]{:S(2)}, u32[]{:S(2)}) %collective-permute-start.2) | collective-permute-done | bytes 65568 | tf_op jit(solution)/shard_map/ppermute | solution.py:246
  56.7 0.0 all-to-all-done.1
  56.7 3.0 %solve.1 = f32[64,8,128]{2,1,0:T(8,128)S(1)} custom-call(f32[2080]{0:T(1024)S(1)} %copy-done.10, f32[2,4,16,128]{3,2,1,0:T(8,128)S(1)} %get-tuple-element.6.m0_ref, f32[2,4,16,128]{3,2,1,0:T(8,128)S(1)} %collective-permute-done.m1_ref, f32[2,4,16,128]{3,2,1,0:T(8,128)S(1)} %collective-permute-done.1.m2_ref, ...), custom_call_target="tpu_custom_call" | custom-call | tf_op jit(solution)/shard_map/solve/pallas_call | solution.py:293
  59.7 0.0 copy-start.4
  59.7 25.7 %all_to_all.21 = f32[256,2,128]{2,1,0:T(2,128)S(1)} all-to-all(f32[256,2,128]{2,1,0:T(2,128)S(1)} %bitcast.11), channel_id=1, replica_groups=mesh['tm'=64,'space'=4] {'tm','space'}, dimensions={0} | all-to-all | bytes 524288 | tf_op jit(solution)/shard_map/all_to_all | solution.py:310
  85.4 0.7 copy-done.11
  86.1 0.1 jit_solution_.3.b_ref
  86.2 0.4 inverse.1
  86.6 0.0 copy-start.1
  86.6 0.0 copy-start.3
  86.6 14.1 %all_to_all.22.d_ref = f32[64,4,128]{2,1,0:T(4,128)S(1)} all-to-all(f32[64,4,128]{2,1,0:T(4,128)S(1)} %inverse.1), channel_id=1, replica_groups=mesh['tm'=64,'space'=4] {'tm'}, dimensions={0} | all-to-all | bytes 262144 | tf_op jit(solution)/shard_map/all_to_all | solution.py:320
  100.7 0.0 copy-done.1
  100.7 0.7 update.1
  (9 shorter events, 0.0 us)
Async XLA Ops:
  0.6 0.8 copy-start
  1.5 0.8 copy-start.2
  2.3 0.8 copy-start.6
  3.2 0.8 copy-start.8
  3.9 0.8 copy-start.9
  4.8 23.7 %copy-start.5 = (f32[128,128]{1,0:T(8,128)S(1)}, f32[128,128]{1,0:T(8,128)}, u32[]{:S(2)}) copy-start(f32[128,128]{1,0:T(8,128)} %constant.8.clone.f_ref) | copy-start | bytes 196612
  4.8 23.7 %copy-start.7 = (f32[4,16,128]{2,1,0:T(8,128)S(1)}, f32[4,16,128]{2,1,0:T(8,128)}, u32[]{:S(2)}) copy-start(f32[4,16,128]{2,1,0:T(8,128)} %param.13) | copy-start | bytes 98308
  29.9 26.7 %copy-start.10 = (f32[2080]{0:T(1024)S(1)}, f32[2080]{0:T(1024)}, u32[]{:S(2)}) copy-start(f32[2080]{0:T(1024)} %constant.9.clone.co_ref) | copy-start | bytes 24964
  29.9 26.7 %all-to-all-start.1 = ((f32[256,2,128]{2,1,0:T(2,128)}), f32[256,2,128]{2,1,0:T(2,128)S(1)}, u32[]{:S(2)}, u32[]{:S(2)}) async-start(f32[256,2,128]{2,1,0:T(2,128)} %bitcast.4), calls=%async_computation.1 | async-start | bytes 524288 | tf_op jit(solution)/shard_map/all_to_all | solution.py:291
  40.1 7.9 %collective-permute-start = (f32[2,4,16,128]{3,2,1,0:T(8,128)S(1)}, f32[2,4,16,128]{3,2,1,0:T(8,128)S(1)}, u32[]{:S(2)}, u32[]{:S(2)}) collective-permute-start(f32[2,4,16,128]{3,2,1,0:T(8,128)S(1)} %get-tuple-element.6.m0_ref), channel_id=1, source_target_pairs={{0,1},{1,0},{2,3},{3,2},{4,5},{5,4},{6,7},{7,6},{8,9},{9,8},{10,11... | collective-permute-start | bytes 196616 | tf_op jit(solution)/shard_map/ppermute | solution.py:246
  42.3 11.9 %collective-permute-start.1 = (f32[2,4,16,128]{3,2,1,0:T(8,128)S(1)}, f32[2,4,16,128]{3,2,1,0:T(8,128)S(1)}, u32[]{:S(2)}, u32[]{:S(2)}) collective-permute-start(f32[2,4,16,128]{3,2,1,0:T(8,128)S(1)} %get-tuple-element.6.m0_ref), channel_id=1, source_target_pairs={{0,2},{1,3},{2,0},{3,1},{4,6},{5,7},{6,4},{7,5},{8,10},{9,11},{10,... | collective-permute-start | bytes 196616 | tf_op jit(solution)/shard_map/ppermute | solution.py:246
  46.8 9.9 %collective-permute-start.2 = (f32[2,4,16,128]{3,2,1,0:T(8,128)S(1)}, f32[2,4,16,128]{3,2,1,0:T(8,128)S(1)}, u32[]{:S(2)}, u32[]{:S(2)}) collective-permute-start(f32[2,4,16,128]{3,2,1,0:T(8,128)S(1)} %get-tuple-element.6.m0_ref), channel_id=1, source_target_pairs={{0,3},{1,2},{2,1},{3,0},{4,7},{5,6},{6,5},{7,4},{8,11},{9,10},{10,... | collective-permute-start | bytes 196616 | tf_op jit(solution)/shard_map/ppermute | solution.py:246
  59.7 26.5 %copy-start.4 = (f32[128,128]{1,0:T(8,128)S(1)}, f32[128,128]{1,0:T(8,128)}, u32[]{:S(2)}) copy-start(f32[128,128]{1,0:T(8,128)} %constant.10.clone.g_ref) | copy-start | bytes 196612
  85.4 0.7 copy-start.11
  86.6 14.1 %copy-start.1 = (f32[2,4,16,128]{3,2,1,0:T(8,128)S(1)}, f32[2,4,16,128]{3,2,1,0:T(8,128)}, u32[]{:S(2)}) copy-start(f32[2,4,16,128]{3,2,1,0:T(8,128)} %param.10) | copy-start | bytes 196612
  86.6 14.1 %copy-start.3 = (f32[2,4,16,128]{3,2,1,0:T(8,128)S(1)}, f32[2,4,16,128]{3,2,1,0:T(8,128)}, u32[]{:S(2)}) copy-start(f32[2,4,16,128]{3,2,1,0:T(8,128)} %param.11) | copy-start | bytes 196612

commit v2 on v1

v2 whole, which is shorter than its diff:
```python
import functools

import jax
import jax.numpy as jnp
import numpy as np
from jax import lax
from jax.experimental import pallas as pl
from jax.experimental.pallas import tpu as pltpu
from jax.sharding import PartitionSpec as P

CHEB = 8
step_rate = 2.0
coupling = 1.0
lower_edge = 0.05
upper_edge = 7.0
COEF = 32
vmem = functools.partial(pl.BlockSpec, memory_space=pltpu.VMEM)
grant = pltpu.CompilerParams(vmem_limit_bytes=8 * 1024 * 1024)
hbm = functools.partial(pl.BlockSpec, memory_space=pltpu.HBM)
smem = functools.partial(pl.BlockSpec, memory_space=pltpu.SMEM)


def time_tables(horizon, slots):
    k = np.arange(slots)[:, None]
    n = np.concatenate([np.arange(0, horizon, 2), np.arange(1, horizon, 2)])[None, :]
    angle = 2.0 * np.pi / horizon * ((k * n) % horizon)
    cosine, sine = np.cos(angle), np.sin(angle)
    alternation = np.where(n % 2 == 0, 1.0, -1.0)
    forward = np.concatenate([cosine, np.where(k == 0, alternation, -sine)], 0)
    inverse = (
        np.concatenate(
            [
                np.where(k == 0, 1.0, 2.0) * cosine,
                np.where(k == 0, alternation, -2.0 * sine),
            ],
            0,
        )
        / horizon
    )
    return forward.astype(np.float32), inverse.T.astype(np.float32)


def solver_table(horizon, slots):
    theta = 2.0 * np.pi / horizon * np.arange(slots + 1)
    shift = step_rate * (1.0 - np.cos(theta))
    twist = step_rate * np.sin(theta)
    twist[slots] = 0.0
    spread = twist * twist + coupling
    lower = (lower_edge + shift) ** 2 + spread
    upper = (upper_edge + shift) ** 2 + spread
    centre = 0.5 * (upper + lower)
    half = 0.5 * (upper - lower)
    ratio = centre / half
    rho = 1.0 / ratio
    table = np.zeros((slots + 1, COEF))
    table[:, 0] = shift
    table[:, 1] = spread
    table[:, 2] = 1.0 / centre
    for step in range(CHEB - 1):
        rho_next = 1.0 / (2.0 * ratio - rho)
        table[:, 4 + 2 * step] = rho_next * rho
        table[:, 5 + 2 * step] = 2.0 * rho_next / half
        rho = rho_next
    return table.reshape(-1).astype(np.float32), twist[:slots]


def twist_block(twist):
    block = np.zeros((twist.shape[0], 128), np.float32)
    block[:, 0] = twist
    return block


def rows_of(count, start, stride):
    return pl.ds(start, count, stride=stride)


def pack_kernel(c_hbm, r_hbm, y_hbm, p_hbm, t_hbm, o_ref, m_ref, y_ref, p_ref, t_ref, sem):
    copies = [
        pltpu.make_async_copy(source, target, sem.at[i])
        for i, (source, target) in enumerate(
            (
                (y_hbm, y_ref),
                (p_hbm, p_ref),
                (t_hbm, t_ref),
                (c_hbm, m_ref.at[0]),
                (r_hbm, m_ref.at[1]),
            )
        )
    ]
    for copy in copies:
        copy.start()
    for copy in copies:
        copy.wait()
    rows = y_ref.shape[1]
    for i, ref in enumerate((y_ref, p_ref, t_ref)):
        for j in range(2):
            o_ref[rows_of(rows, 2 * i + j, 6), :] = ref[j]


def halves(value):
    high = value.astype(jnp.bfloat16)
    return high, (value - high.astype(jnp.float32)).astype(jnp.bfloat16)


def product(high, low, data):
    data_high, data_low = halves(data)
    dot = functools.partial(lax.dot, preferred_element_type=jnp.float32)
    return dot(high, data_high) + (dot(high, data_low) + dot(low, data_high))


def forward_kernel(fh_ref, fl_ref, init_ref, x_ref, o_ref):
    rows = x_ref.shape[0] // 6
    lanes = x_ref.shape[1]
    mine = lax.axis_index("tm")
    y0, y1, p0, p1, t0, t1 = (x_ref[rows_of(rows, i, 6), :] for i in range(6))
    g0, g1 = (y * y * y * (1.0 / 3.0) + coupling * p for y, p in ((y0, p0), (y1, p1)))
    h0, h1 = (y * y * p - y + t for y, p, t in ((y0, p0, t0), (y1, p1, t1)))
    row = lax.broadcasted_iota(jnp.int32, (rows, lanes), 0)
    before = jnp.where(row == 0, init_ref[pl.ds(mine, 1), :], pltpu.roll(y1, 1, 0))
    after = jnp.where(row == rows - 1, 0.0, pltpu.roll(p0, rows - 1, 0))
    a0 = g0 + step_rate * (y0 - before)
    a1 = g1 + step_rate * (y1 - y0)
    b0 = h0 + step_rate * (p0 - p1)
    b1 = h1 + step_rate * (p1 - after)
    data = jnp.concatenate(
        [
            jnp.concatenate([a0, b0, y0, p0], 1),
            jnp.concatenate([a1, b1, y1, p1], 1),
        ],
        0,
    )
    hat = product(fh_ref[...], fl_ref[...], data)
    for f in range(2):
        for r in range(2):
            for q in range(2):
                column = (q * 2 + f) * lanes
                o_ref[rows_of(rows, (f * 2 + r) * 2 * rows + q, 2), :] = hat[
                    r * rows : (r + 1) * rows, column : column + lanes
                ]


def faces_kernel(m0_ref, m1_ref, m2_ref, m3_ref, cx, cyp, cym, czp, czm, bare, both, mat):
    item = lax.axis_index("space")
    for piece, ref in enumerate((m0_ref, m1_ref, m2_ref, m3_ref)):
        mat[item ^ piece] = ref[...]
    slabs, _, width, count_y, lanes = mat.shape
    count = slabs * width
    row = lax.broadcasted_iota(jnp.int32, (count_y, lanes), 0)
    lane = lax.broadcasted_iota(jnp.int32, (count_y, lanes), 1)

    def cond(x):
        return mat[x // width, 0, x % width]

    for x in range(count):
        c = cond(x)
        half = 0.5 * c
        up = 0.5 * (c + cond(x + 1)) if x + 1 < count else half
        down = 0.5 * (c + cond(x - 1)) if x > 0 else half
        cx[x] = up
        yp = jnp.where(row == count_y - 1, 0.0, 0.5 * pltpu.roll(c, count_y - 1, 0)) + half
        ym = jnp.where(row == 0, 0.0, 0.5 * pltpu.roll(c, 1, 0)) + half
        zp = jnp.where(lane == lanes - 1, 0.0, 0.5 * pltpu.roll(c, lanes - 1, 1)) + half
        zm = jnp.where(lane == 0, 0.0, 0.5 * pltpu.roll(c, 1, 1)) + half
        total = (up + down) + (yp + ym) + (zp + zm)
        bare[x] = total
        both[x] = total + mat[x // width, 1, x % width]
        cyp[x] = jnp.where(row == count_y - 1, 0.0, yp)
        cym[x] = jnp.where(row == 0, 0.0, ym)
        czp[x] = jnp.where(lane == lanes - 1, 0.0, zp)
        czm[x] = jnp.where(lane == 0, 0.0, zm)


def solve_kernel(co_ref, cx, cyp, cym, czp, czm, bare, both, x_ref, o_ref, diag, yy, res, d, t, w):
    slot = lax.axis_index("tm")
    item = lax.axis_index("space")
    cells = x_ref.shape[0] // 8
    slots = cells
    frequency = jnp.where((slot == 0) & (item % 2 == 1), slots, slot)
    base = frequency * COEF
    shift = co_ref[base]
    spread = co_ref[base + 1]
    start = co_ref[base + 2]
    slabs = 4
    count, count_y, lanes = d.shape
    width = count // slabs
    for s in range(slabs):
        res[s * width : (s + 1) * width] = x_ref[rows_of(cells, 2 * s * cells, 2), :].reshape(width, count_y, lanes)
        yy[s * width : (s + 1) * width] = x_ref[rows_of(cells, 2 * s * cells + 1, 2), :].reshape(width, count_y, lanes)

    def applied(ref, x, centre):
        v = ref[x]
        out = centre * v
        if x + 1 < count:
            out = out - cx[x] * ref[x + 1]
        if x > 0:
            out = out - cx[x - 1] * ref[x - 1]
        out = out - cyp[x] * pltpu.roll(v, count_y - 1, 0)
        out = out - cym[x] * pltpu.roll(v, 1, 0)
        out = out - czp[x] * pltpu.roll(v, lanes - 1, 1)
        out = out - czm[x] * pltpu.roll(v, 1, 1)
        return out

    for x in range(count):
        diag[x] = both[x] + shift
        r = res[x] + applied(yy, x, bare[x])
        first = start * r
        res[x] = r
        d[x] = first
        w[x] = first

    def step(i, carry):
        alpha = co_ref[base + 4 + 2 * i]
        beta = co_ref[base + 5 + 2 * i]
        for x in range(count):
            t[x] = applied(d, x, diag[x])
        for x in range(count):
            now = d[x]
            r = res[x] - (applied(t, x, diag[x]) + spread * now)
            now = alpha * now + beta * r
            res[x] = r
            d[x] = now
            w[x] = w[x] + now
        return carry

    lax.fori_loop(0, CHEB - 1, step, 0)
    for x in range(count):
        t[x] = applied(w, x, diag[x])
    for s in range(slabs):
        o_ref[rows_of(cells, 2 * s * cells, 2), :] = w[s * width : (s + 1) * width].reshape(width * count_y, lanes)
        o_ref[rows_of(cells, 2 * s * cells + 1, 2), :] = t[s * width : (s + 1) * width].reshape(width * count_y, lanes)


def inverse_kernel(gh_ref, gl_ref, b_ref, x_ref, o_ref):
    rows = x_ref.shape[0] // 8
    lanes = x_ref.shape[1]
    b = jnp.broadcast_to(b_ref[:, 0:1], (rows, lanes))
    u_re, ku_re, u_im, ku_im, v_re, kv_re, v_im, kv_im = (
        x_ref[rows_of(rows, i // 2 * 2 * rows + i % 2, 2), :] for i in range(8)
    )
    c00 = ku_re - (coupling * v_re - b * u_im)
    c01 = ku_im - (coupling * v_im + b * u_re)
    c10 = kv_re - (b * v_im - u_re)
    c11 = kv_im + (b * v_re + u_im)
    data = jnp.concatenate(
        [jnp.concatenate([c00, c10], 1), jnp.concatenate([c01, c11], 1)],
        0,
    )
    back = product(gh_ref[...], gl_ref[...], data)
    for f in range(2):
        for j in range(2):
            o_ref[rows_of(rows, f * 2 + j, 4), :] = back[
                j * rows : (j + 1) * rows, f * lanes : (f + 1) * lanes
            ]


def update_kernel(y_ref, p_ref, d_ref, ny_ref, np_ref):
    rows = y_ref.shape[1]
    for j in range(2):
        ny_ref[j] = y_ref[j] - d_ref[rows_of(rows, j, 4), :]
        np_ref[j] = p_ref[j] - d_ref[rows_of(rows, 2 + j, 4), :]


def swapped(value, distance):
    count = lax.axis_size("space")
    return lax.ppermute(value, "space", [(i, i ^ distance) for i in range(count)])


def shards(state_field, adjoint, target, initial_state, conductivity, reaction):
    steps, width_x, width_y, width_z = state_field.shape
    devices = lax.axis_size("tm")
    spaces = lax.axis_size("space")
    rows = width_x * width_y
    horizon = steps * devices
    assert steps == 2 and rows == devices and spaces == 4
    f32 = jnp.float32

    def shape(*dims):
        return jax.ShapeDtypeStruct(dims, f32)

    flat = (steps, rows, width_z)
    state_rows = state_field.reshape(flat)
    adjoint_rows = adjoint.reshape(flat)
    packed, material = pl.pallas_call(
        pack_kernel,
        out_shape=(
            shape(rows * 6, width_z),
            shape(2, width_x, width_y, width_z),
        ),
        in_specs=[hbm()] * 5,
        out_specs=(vmem(), vmem()),
        scratch_shapes=[pltpu.VMEM(flat, f32)] * 3 + [pltpu.SemaphoreType.DMA((5,))],
        name="pack",
    )(conductivity, reaction, state_rows, adjoint_rows, target.reshape(flat))
    table, twist = solver_table(horizon, devices)
    material_far = swapped(material, 2)
    material_core = swapped(material, 1)
    by_cell = lax.all_to_all(
        packed.reshape(rows * 3, 2, width_z), "tm", 0, 0, tiled=True
    ).reshape(packed.shape)
    by_cell, material_far = lax.optimization_barrier((by_cell, material_far))
    material_both = swapped(material_far, 1)
    forward, inverse = (halves(jnp.asarray(each)) for each in time_tables(horizon, devices))
    hat = pl.pallas_call(
        forward_kernel,
        out_shape=shape(devices * 8, width_z),
        in_specs=[vmem()] * 4,
        out_specs=vmem(),
        compiler_params=grant,
        name="forward",
    )(*forward, initial_state.reshape(rows, width_z), by_cell)
    everyone = ("space", "tm")
    by_item = lax.all_to_all(hat, everyone, 0, 0, tiled=True)
    grid = (spaces * width_x, width_y, width_z)
    faces = pl.pallas_call(
        faces_kernel,
        out_shape=(shape(*grid),) * 7,
        in_specs=[vmem()] * 4,
        out_specs=(vmem(),) * 7,
        scratch_shapes=[pltpu.VMEM((spaces, 2, width_x, width_y, width_z), f32)],
        compiler_params=grant,
        name="faces",
    )(material, material_core, material_far, material_both)
    solved = pl.pallas_call(
        solve_kernel,
        out_shape=shape(rows * 8, width_z),
        in_specs=[smem()] + [vmem()] * 8,
        out_specs=vmem(),
        scratch_shapes=[pltpu.VMEM(grid, f32)] * 6,
        compiler_params=grant,
        name="solve",
    )(jnp.asarray(table), *faces, by_item)
    by_row = lax.all_to_all(solved, everyone, 0, 0, tiled=True)
    delta = pl.pallas_call(
        inverse_kernel,
        out_shape=shape(devices * 4, width_z),
        in_specs=[vmem()] * 4,
        out_specs=vmem(),
        compiler_params=grant,
        name="inverse",
    )(*inverse, jnp.asarray(twist_block(twist)), by_row)
    by_time = lax.all_to_all(delta, "tm", 0, 0, tiled=True)
    new_state, new_adjoint = pl.pallas_call(
        update_kernel,
        out_shape=(shape(*flat), shape(*flat)),
        in_specs=[vmem()] * 3,
        out_specs=(vmem(), vmem()),
        compiler_params=grant,
        name="update",
    )(state_rows, adjoint_rows, by_time)
    return new_state.reshape(state_field.shape), new_adjoint.reshape(adjoint.shape)


def solution(mesh):
    in_specs = (
        P("tm", "space", None, None),
        P("tm", "space", None, None),
        P("tm", "space", None, None),
        P("space", None, None),
        P("space", None, None),
        P("space", None, None),
    )
    out_specs = (P("tm", "space", None, None), P("tm", "space", None, None))
    return jax.shard_map(shards, mesh=mesh, in_specs=in_specs, out_specs=out_specs, check_vma=False)
```

time: 102 us -> 92.3 us (0.905)
  blocking collectives: 63.5 us -> 35 us
  starting transfers between devices: 18 us -> 31.2 us
  waiting for transfers between devices: 8.7 us -> 18.5 us
  local copies, waits for them, and re-layouts: 4.79 us -> 0.07 us
    all_to_all x2 -> x1, blocking collectives: 49.4 us -> 20.4 us  [shards(): by_row = lax.all_to_all(solved, everyone, 0, 0, tiled=True)]
    all_to_all x1 -> x2, starting transfers between devices: 10.1 us -> 24.5 us  [the longest x1 12.7 us: shards(): lax.all_to_all(packed.reshape(rows * 3, 2, width_z), 'tm', 0, 0, tiled=True)]
    all_to_all x1 -> x2, waiting for transfers between devices: 0.01 us -> 13.1 us  [the longest x1 11.5 us: shards(): by_item = lax.all_to_all(hat, everyone, 0, 0, tiled=True)]
    unnamed x24 -> x20, local copies, waits for them, and re-layouts: 4.72 us -> 0.07 us
    ppermute x3, waiting for transfers between devices: 8.7 us -> 5.45 us  [swapped(): lax.ppermute(value, 'space', [(i, i ^ distance) for i in range(count)])]
    ppermute x3, starting transfers between devices: 7.87 us -> 6.63 us  [swapped(): lax.ppermute(value, 'space', [(i, i ^ distance) for i in range(count)])]
    pallas_call x4 -> x5, Pallas kernels: 5 us -> 5.76 us  [the longest x1 2.72 us: shards(): pl.pallas_call(solve_kernel, out_shape=shape(rows * 8, width_z), in_specs...]
  transfers between devices with their start and end apart: 4 -> 5, of which waited for: 2 -> 5; matrix products, arithmetic and copies ran while one was open for 0% -> 0% of each run, Pallas kernels for 0% -> 0%
where the time goes in v2:
time: 92.3 us; the launch traced here: 91.9 us
  blocking collectives  35 us (38%)
  starting transfers between devices  31.2 us (34%)
  waiting for transfers between devices  18.5 us (20%)
  Pallas kernels  6.43 us (7%)
    all_to_all x1, blocking collectives, shards(): by_row = lax.all_to_all(solved, everyone, 0, 0, tiled=True)  20.4 us
    all_to_all x1, blocking collectives, shards(): by_time = lax.all_to_all(delta, 'tm', 0, 0, tiled=True)  14.6 us
    all_to_all x1, starting transfers between devices, shards(): lax.all_to_all(packed.reshape(rows * 3, 2, width_z), 'tm', 0, 0, tiled=True)  12.7 us
    all_to_all x1, starting transfers between devices, shards(): by_item = lax.all_to_all(hat, everyone, 0, 0, tiled=True)  11.8 us
    all_to_all x1, waiting for transfers between devices, shards(): by_item = lax.all_to_all(hat, everyone, 0, 0, tiled=True)  11.5 us
    ppermute x3, starting transfers between devices, swapped(): lax.ppermute(value, 'space', [(i, i ^ distance) for i in range(count)])  6.63 us
    ppermute x3, waiting for transfers between devices, swapped(): lax.ppermute(value, 'space', [(i, i ^ distance) for i in range(count)])  5.45 us
    pallas_call x1, Pallas kernels, shards(): pl.pallas_call(solve_kernel, out_shape=shape(rows * 8, width_z), in_specs...  2.72 us
  transfers between devices with their start and end apart: 5, of which 5 were waited for; matrix products, arithmetic and copies ran while one was open for 0% of the time, Pallas kernels for 0%

profile of v2, /device:TPU:1, one launch (start us, length us, event | category | flops | bytes accessed | tf_op | source)
XLA Modules:
  0.0 91.9 jit_solution(6058165128034672177)
XLA Ops:
  0.6 1.6 %pack.1 = (f32[384,128]{1,0:T(8,128)}, f32[2,4,16,128]{3,2,1,0:T(8,128)}) custom-call(f32[4,16,128]{2,1,0:T(8,128)} %c_hbm.1, f32[4,16,128]{2,1,0:T(8,128)} %r_hbm.1, f32[2,64,128]{2,1,0:T(8,128)} %bitcast.20, f32[2,64,128]{2,1,0:T(8,128)} %bitcast.22, f32[2,64,128]{2,1,0:T(8,128)} %bitcast.26), custom_call_target="tpu_custom_call" | custom-call | tf_op jit(solution)/shard_map/pack/pallas_call | solution.py:283
  2.3 0.0 copy-start.2
  2.3 0.0 copy-start.3
  2.3 0.0 copy-start.4
  2.3 0.0 copy-start.5
  2.3 12.7 %all-to-all-start = ((f32[192,2,128]{2,1,0:T(2,128)}), f32[192,2,128]{2,1,0:T(2,128)S(1)}, u32[]{:S(2)}, u32[]{:S(2)}) async-start(f32[192,2,128]{2,1,0:T(2,128)} %bitcast.25), calls=%async_computation | async-start | bytes 393216 | tf_op jit(solution)/shard_map/all_to_all | solution.py:297
  15.0 4.3 %collective-permute-start.1 = (f32[2,4,16,128]{3,2,1,0:T(8,128)S(1)}, f32[2,4,16,128]{3,2,1,0:T(8,128)S(1)}, u32[]{:S(2)}, u32[]{:S(2)}) collective-permute-start(f32[2,4,16,128]{3,2,1,0:T(8,128)S(1)} %copy-done.2), channel_id=1, source_target_pairs={{0,2},{1,3},{2,0},{3,1},{4,6},{5,7},{6,4},{7,5},{8,10},{9,11},{10,... | collective-permute-start | bytes 196616 | tf_op jit(solution)/shard_map/ppermute | solution.py:265
  19.3 4.3 %collective-permute-done.1.m2_ref = f32[2,4,16,128]{3,2,1,0:T(8,128)S(1)} collective-permute-done((f32[2,4,16,128]{3,2,1,0:T(8,128)S(1)}, f32[2,4,16,128]{3,2,1,0:T(8,128)S(1)}, u32[]{:S(2)}, u32[]{:S(2)}) %collective-permute-start.1) | collective-permute-done | bytes 65568 | tf_op jit(solution)/shard_map/ppermute | solution.py:265
  23.6 1.6 %all-to-all-done = f32[192,2,128]{2,1,0:T(2,128)S(1)} async-done(((f32[192,2,128]{2,1,0:T(2,128)}), f32[192,2,128]{2,1,0:T(2,128)S(1)}, u32[]{:S(2)}, u32[]{:S(2)}) %all-to-all-start) | async-done | bytes 196640 | tf_op jit(solution)/shard_map/all_to_all | solution.py:297
  25.3 0.0 copy-done.5
  25.3 1.0 %forward.1 = f32[512,128]{1,0:T(8,128)} custom-call(bf16[128,128]{1,0:T(8,128)(2,1)S(1)} %copy-done.5, bf16[128,128]{1,0:T(8,128)(2,1)S(1)} %copy-done.4, f32[64,128]{1,0:T(8,128)S(1)} %bitcast.24, f32[384,128]{1,0:T(8,128)S(1)} %bitcast.17), custom_call_target="tpu_custom_call" | custom-call | tf_op jit(solution)/shard_map/forward/pallas_call | solution.py:303
  26.2 11.8 %all-to-all-start.1 = ((f32[256,2,128]{2,1,0:T(2,128)}), f32[256,2,128]{2,1,0:T(2,128)S(1)}, u32[]{:S(2)}, u32[]{:S(2)}) async-start(f32[256,2,128]{2,1,0:T(2,128)} %bitcast.6), calls=%async_computation.1 | async-start | bytes 524288 | tf_op jit(solution)/shard_map/all_to_all | solution.py:312
  38.1 2.2 %collective-permute-start = (f32[2,4,16,128]{3,2,1,0:T(8,128)S(1)}, f32[2,4,16,128]{3,2,1,0:T(8,128)S(1)}, u32[]{:S(2)}, u32[]{:S(2)}) collective-permute-start(f32[2,4,16,128]{3,2,1,0:T(8,128)S(1)} %copy-done.2), channel_id=1, source_target_pairs={{0,1},{1,0},{2,3},{3,2},{4,5},{5,4},{6,7},{7,6},{8,9},{9,8},{10,11... | collective-permute-start | bytes 196616 | tf_op jit(solution)/shard_map/ppermute | solution.py:265
  40.3 0.1 collective-permute-start.2
  40.4 0.8 collective-permute-done.m1_ref
  41.2 0.4 collective-permute-done.2.m3_ref
  41.6 0.2 faces.1
  41.7 0.0 copy-start.9
  41.7 11.5 %all-to-all-done.1 = f32[256,2,128]{2,1,0:T(2,128)S(1)} async-done(((f32[256,2,128]{2,1,0:T(2,128)}), f32[256,2,128]{2,1,0:T(2,128)S(1)}, u32[]{:S(2)}, u32[]{:S(2)}) %all-to-all-start.1) | async-done | bytes 262176 | tf_op jit(solution)/shard_map/all_to_all | solution.py:312
  53.2 2.7 %solve.1 = f32[512,128]{1,0:T(8,128)S(1)} custom-call(f32[2080]{0:T(1024)S(1)} %copy-done.9, f32[16,16,128]{2,1,0:T(8,128)S(1)} %get-tuple-element.18.cx, f32[16,16,128]{2,1,0:T(8,128)S(1)} %get-tuple-element.19.cyp, f32[16,16,128]{2,1,0:T(8,128)S(1)} %get-tuple-element.20.cym, f32[16,16,128]{2,1,0:T(8,128)S(1)} %get-tuple-element.21.czp, ...), custom_call_target="tpu_custom_call" | custom-call | tf_op jit(solution)/shard_map/solve/pallas_call | solution.py:323
  55.9 0.0 copy-start.6
  55.9 0.0 copy-start.7
  56.0 0.0 copy-start.8
  56.0 20.4 %all_to_all.38 = f32[256,2,128]{2,1,0:T(2,128)S(1)} all-to-all(f32[256,2,128]{2,1,0:T(2,128)S(1)} %bitcast.16), channel_id=1, replica_groups=mesh['tm'=64,'space'=4] {'space','tm'}, dimensions={0} | all-to-all | bytes 524288 | tf_op jit(solution)/shard_map/all_to_all | solution.py:332
  76.3 0.0 copy-done.6
  76.3 0.0 copy-done.8
  76.3 0.3 inverse.1
  76.6 0.0 copy-start
  76.6 0.0 copy-start.1
  76.7 14.6 %all_to_all.39 = f32[64,4,128]{2,1,0:T(4,128)S(1)} all-to-all(f32[64,4,128]{2,1,0:T(4,128)S(1)} %bitcast.19), channel_id=1, replica_groups=mesh['tm'=64,'space'=4] {'tm'}, dimensions={0} | all-to-all | bytes 262144 | tf_op jit(solution)/shard_map/all_to_all | solution.py:341
  91.3 0.0 copy-done.1
  91.3 0.7 update.1
  (6 shorter events, 0.0 us)
Async XLA Ops:
  2.3 12.7 %copy-start.2 = (f32[2,4,16,128]{3,2,1,0:T(8,128)S(1)}, f32[2,4,16,128]{3,2,1,0:T(8,128)}, u32[]{:S(2)}) copy-start(f32[2,4,16,128]{3,2,1,0:T(8,128)} %get-tuple-element.15.m0_ref) | copy-start | bytes 196612
  2.3 23.0 %copy-start.3 = (f32[4,16,128]{2,1,0:T(8,128)S(1)}, f32[4,16,128]{2,1,0:T(8,128)}, u32[]{:S(2)}) copy-start(f32[4,16,128]{2,1,0:T(8,128)} %param.13) | copy-start | bytes 98308
  2.3 23.0 %copy-start.4 = (bf16[128,128]{1,0:T(8,128)(2,1)S(1)}, bf16[128,128]{1,0:T(8,128)(2,1)}, u32[]{:S(2)}) copy-start(bf16[128,128]{1,0:T(8,128)(2,1)} %constant.22.fl_ref) | copy-start | bytes 98308
  2.3 22.9 %copy-start.5 = (bf16[128,128]{1,0:T(8,128)(2,1)S(1)}, bf16[128,128]{1,0:T(8,128)(2,1)}, u32[]{:S(2)}) copy-start(bf16[128,128]{1,0:T(8,128)(2,1)} %constant.19.fh_ref) | copy-start | bytes 98308
  2.3 22.9 %all-to-all-start = ((f32[192,2,128]{2,1,0:T(2,128)}), f32[192,2,128]{2,1,0:T(2,128)S(1)}, u32[]{:S(2)}, u32[]{:S(2)}) async-start(f32[192,2,128]{2,1,0:T(2,128)} %bitcast.25), calls=%async_computation | async-start | bytes 393216 | tf_op jit(solution)/shard_map/all_to_all | solution.py:297
  15.0 8.6 %collective-permute-start.1 = (f32[2,4,16,128]{3,2,1,0:T(8,128)S(1)}, f32[2,4,16,128]{3,2,1,0:T(8,128)S(1)}, u32[]{:S(2)}, u32[]{:S(2)}) collective-permute-start(f32[2,4,16,128]{3,2,1,0:T(8,128)S(1)} %copy-done.2), channel_id=1, source_target_pairs={{0,2},{1,3},{2,0},{3,1},{4,6},{5,7},{6,4},{7,5},{8,10},{9,11},{10,... | collective-permute-start | bytes 196616 | tf_op jit(solution)/shard_map/ppermute | solution.py:265
  26.2 27.0 %all-to-all-start.1 = ((f32[256,2,128]{2,1,0:T(2,128)}), f32[256,2,128]{2,1,0:T(2,128)S(1)}, u32[]{:S(2)}, u32[]{:S(2)}) async-start(f32[256,2,128]{2,1,0:T(2,128)} %bitcast.6), calls=%async_computation.1 | async-start | bytes 524288 | tf_op jit(solution)/shard_map/all_to_all | solution.py:312
  38.1 3.1 %collective-permute-start = (f32[2,4,16,128]{3,2,1,0:T(8,128)S(1)}, f32[2,4,16,128]{3,2,1,0:T(8,128)S(1)}, u32[]{:S(2)}, u32[]{:S(2)}) collective-permute-start(f32[2,4,16,128]{3,2,1,0:T(8,128)S(1)} %copy-done.2), channel_id=1, source_target_pairs={{0,1},{1,0},{2,3},{3,2},{4,5},{5,4},{6,7},{7,6},{8,9},{9,8},{10,11... | collective-permute-start | bytes 196616 | tf_op jit(solution)/shard_map/ppermute | solution.py:265
  40.3 1.3 %collective-permute-start.2 = (f32[2,4,16,128]{3,2,1,0:T(8,128)S(1)}, f32[2,4,16,128]{3,2,1,0:T(8,128)S(1)}, u32[]{:S(2)}, u32[]{:S(2)}) collective-permute-start(f32[2,4,16,128]{3,2,1,0:T(8,128)S(1)} %collective-permute-done.1.m2_ref), channel_id=1, source_target_pairs={{0,1},{1,0},{2,3},{3,2},{4,5},{5,4},{6,7},{7,6},{8,9},{9,8},{10,11... | collective-permute-start | bytes 196616 | tf_op jit(solution)/shard_map/ppermute | solution.py:265
  41.7 11.5 %copy-start.9 = (f32[2080]{0:T(1024)S(1)}, f32[2080]{0:T(1024)}, u32[]{:S(2)}) copy-start(f32[2080]{0:T(1024)} %constant.10.clone.co_ref) | copy-start | bytes 24964
  55.9 20.4 %copy-start.6 = (bf16[128,128]{1,0:T(8,128)(2,1)S(1)}, bf16[128,128]{1,0:T(8,128)(2,1)}, u32[]{:S(2)}) copy-start(bf16[128,128]{1,0:T(8,128)(2,1)} %constant.18.gl_ref) | copy-start | bytes 98308
  55.9 20.4 %copy-start.7 = (bf16[128,128]{1,0:T(8,128)(2,1)S(1)}, bf16[128,128]{1,0:T(8,128)(2,1)}, u32[]{:S(2)}) copy-start(bf16[128,128]{1,0:T(8,128)(2,1)} %constant.15.gh_ref) | copy-start | bytes 98308
  56.0 20.4 %copy-start.8 = (f32[64,128]{1,0:T(8,128)S(1)}, f32[64,128]{1,0:T(8,128)}, u32[]{:S(2)}) copy-start(f32[64,128]{1,0:T(8,128)} %constant.11.clone.b_ref) | copy-start | bytes 98308
  76.6 14.6 %copy-start = (f32[2,4,16,128]{3,2,1,0:T(8,128)S(1)}, f32[2,4,16,128]{3,2,1,0:T(8,128)}, u32[]{:S(2)}) copy-start(f32[2,4,16,128]{3,2,1,0:T(8,128)} %param.10) | copy-start | bytes 196612
  76.6 14.6 %copy-start.1 = (f32[2,4,16,128]{3,2,1,0:T(8,128)S(1)}, f32[2,4,16,128]{3,2,1,0:T(8,128)}, u32[]{:S(2)}) copy-start(f32[2,4,16,128]{3,2,1,0:T(8,128)} %param.11) | copy-start | bytes 196612

commit v3 on v2

--- a/solution.py
+++ b/solution.py
@@ -308,8 +308,6 @@
         compiler_params=grant,
         name="forward",
     )(*forward, initial_state.reshape(rows, width_z), by_cell)
-    everyone = ("space", "tm")
-    by_item = lax.all_to_all(hat, everyone, 0, 0, tiled=True)
     grid = (spaces * width_x, width_y, width_z)
     faces = pl.pallas_call(
         faces_kernel,
@@ -320,6 +318,9 @@
         compiler_params=grant,
         name="faces",
     )(material, material_core, material_far, material_both)
+    hat, faces = lax.optimization_barrier((hat, faces))
+    everyone = ("space", "tm")
+    by_item = lax.all_to_all(hat, everyone, 0, 0, tiled=True)
     solved = pl.pallas_call(
         solve_kernel,
         out_shape=shape(rows * 8, width_z),

time: 92.3 us -> 92.7 us (level)
  blocking collectives: 35 us -> 59.9 us
  waiting for transfers between devices: 18.5 us -> 5.31 us
  starting transfers between devices: 31.2 us -> 20.4 us
    all_to_all x0 -> x1, blocking collectives: none -> 24.9 us  [shards(): by_item = lax.all_to_all(hat, everyone, 0, 0, tiled=True)]
    all_to_all x1 -> x0, starting transfers between devices: 11.8 us -> none  [shards(): by_item = lax.all_to_all(hat, everyone, 0, 0, tiled=True)]
    all_to_all x1 -> x0, waiting for transfers between devices: 11.5 us -> none  [shards(): by_item = lax.all_to_all(hat, everyone, 0, 0, tiled=True)]
    ppermute x3, waiting for transfers between devices: 5.45 us -> 3.69 us  [swapped(): lax.ppermute(value, 'space', [(i, i ^ distance) for i in range(count)])]
    ppermute x3, starting transfers between devices: 6.63 us -> 7.74 us  [swapped(): lax.ppermute(value, 'space', [(i, i ^ distance) for i in range(count)])]
  transfers between devices with their start and end apart: 5 -> 4, of which waited for: 5 -> 3; matrix products, arithmetic and copies ran while one was open for 0% -> 0% of each run, Pallas kernels for 0% -> 0%
where the time goes in v3:
time: 92.7 us; the launch traced here: 92.2 us
  blocking collectives  59.9 us (65%)
  starting transfers between devices  20.4 us (22%)
  Pallas kernels  5.74 us (6%)
  waiting for transfers between devices  5.31 us (6%)
    all_to_all x1, blocking collectives, shards(): by_item = lax.all_to_all(hat, everyone, 0, 0, tiled=True)  24.9 us
    all_to_all x1, blocking collectives, shards(): by_row = lax.all_to_all(solved, everyone, 0, 0, tiled=True)  20.4 us
    all_to_all x1, blocking collectives, shards(): by_time = lax.all_to_all(delta, 'tm', 0, 0, tiled=True)  14.6 us
    all_to_all x1, starting transfers between devices, shards(): lax.all_to_all(packed.reshape(rows * 3, 2, width_z), 'tm', 0, 0, tiled=True)  12.7 us
    ppermute x3, starting transfers between devices, swapped(): lax.ppermute(value, 'space', [(i, i ^ distance) for i in range(count)])  7.74 us
    ppermute x3, waiting for transfers between devices, swapped(): lax.ppermute(value, 'space', [(i, i ^ distance) for i in range(count)])  3.69 us
    pallas_call x1, Pallas kernels, shards(): pl.pallas_call(solve_kernel, out_shape=shape(rows * 8, width_z), in_specs...  2.72 us
  transfers between devices with their start and end apart: 4, of which 3 were waited for; matrix products, arithmetic and copies ran while one was open for 0% of the time, Pallas kernels for 0%

profile of v3, /device:TPU:1, one launch (start us, length us, event | category | flops | bytes accessed | tf_op | source)
XLA Modules:
  0.0 92.2 jit_solution(11249053496764688218)
XLA Ops:
  0.6 1.6 %pack.1 = (f32[384,128]{1,0:T(8,128)}, f32[2,4,16,128]{3,2,1,0:T(8,128)}) custom-call(f32[4,16,128]{2,1,0:T(8,128)} %c_hbm.1, f32[4,16,128]{2,1,0:T(8,128)} %r_hbm.1, f32[2,64,128]{2,1,0:T(8,128)} %bitcast.21, f32[2,64,128]{2,1,0:T(8,128)} %bitcast.23, f32[2,64,128]{2,1,0:T(8,128)} %bitcast.27), custom_call_target="tpu_custom_call" | custom-call | tf_op jit(solution)/shard_map/pack/pallas_call | solution.py:283
  2.3 0.0 copy-start.2
  2.3 0.0 copy-start.3
  2.3 0.0 copy-start.4
  2.3 0.0 copy-start.5
  2.3 12.7 %all-to-all-start = ((f32[192,2,128]{2,1,0:T(2,128)}), f32[192,2,128]{2,1,0:T(2,128)S(1)}, u32[]{:S(2)}, u32[]{:S(2)}) async-start(f32[192,2,128]{2,1,0:T(2,128)} %bitcast.26), calls=%async_computation | async-start | bytes 393216 | tf_op jit(solution)/shard_map/all_to_all | solution.py:297
  15.0 0.0 copy-done.2
  15.0 4.3 %collective-permute-start = (f32[2,4,16,128]{3,2,1,0:T(8,128)S(1)}, f32[2,4,16,128]{3,2,1,0:T(8,128)S(1)}, u32[]{:S(2)}, u32[]{:S(2)}) collective-permute-start(f32[2,4,16,128]{3,2,1,0:T(8,128)S(1)} %copy-done.2), channel_id=1, source_target_pairs={{0,2},{1,3},{2,0},{3,1},{4,6},{5,7},{6,4},{7,5},{8,10},{9,11},{10,... | collective-permute-start | bytes 196616 | tf_op jit(solution)/shard_map/ppermute | solution.py:265
  19.3 1.2 %collective-permute-start.1 = (f32[2,4,16,128]{3,2,1,0:T(8,128)S(1)}, f32[2,4,16,128]{3,2,1,0:T(8,128)S(1)}, u32[]{:S(2)}, u32[]{:S(2)}) collective-permute-start(f32[2,4,16,128]{3,2,1,0:T(8,128)S(1)} %copy-done.2), channel_id=1, source_target_pairs={{0,1},{1,0},{2,3},{3,2},{4,5},{5,4},{6,7},{7,6},{8,9},{9,8},{10,11... | collective-permute-start | bytes 196616 | tf_op jit(solution)/shard_map/ppermute | solution.py:265
  20.6 3.1 %collective-permute-done.m2_ref = f32[2,4,16,128]{3,2,1,0:T(8,128)S(1)} collective-permute-done((f32[2,4,16,128]{3,2,1,0:T(8,128)S(1)}, f32[2,4,16,128]{3,2,1,0:T(8,128)S(1)}, u32[]{:S(2)}, u32[]{:S(2)}) %collective-permute-start) | collective-permute-done | bytes 65568 | tf_op jit(solution)/shard_map/ppermute | solution.py:265
  23.6 1.6 %all-to-all-done = f32[192,2,128]{2,1,0:T(2,128)S(1)} async-done(((f32[192,2,128]{2,1,0:T(2,128)}), f32[192,2,128]{2,1,0:T(2,128)S(1)}, u32[]{:S(2)}, u32[]{:S(2)}) %all-to-all-start) | async-done | bytes 196640 | tf_op jit(solution)/shard_map/all_to_all | solution.py:297
  25.3 2.2 %collective-permute-start.2 = (f32[2,4,16,128]{3,2,1,0:T(8,128)S(1)}, f32[2,4,16,128]{3,2,1,0:T(8,128)S(1)}, u32[]{:S(2)}, u32[]{:S(2)}) collective-permute-start(f32[2,4,16,128]{3,2,1,0:T(8,128)S(1)} %collective-permute-done.m2_ref), channel_id=1, source_target_pairs={{0,1},{1,0},{2,3},{3,2},{4,5},{5,4},{6,7},{7,6},{8,9},{9,8},{10,11... | collective-permute-start | bytes 196616 | tf_op jit(solution)/shard_map/ppermute | solution.py:265
  27.5 0.0 copy-done.3
  27.5 0.0 copy-done.4
  27.5 0.0 copy-done.5
  27.5 0.3 forward.1
  27.7 0.0 collective-permute-done.1.m1_ref
  27.7 0.6 collective-permute-done.2.m3_ref
  28.4 0.2 faces.1
  28.5 0.0 copy-start.9
  28.5 24.9 %all_to_all.38 = f32[256,2,128]{2,1,0:T(2,128)S(1)} all-to-all(f32[256,2,128]{2,1,0:T(2,128)S(1)} %bitcast.14), channel_id=1, replica_groups=mesh['tm'=64,'space'=4] {'space','tm'}, dimensions={0} | all-to-all | bytes 524288 | tf_op jit(solution)/shard_map/all_to_all | solution.py:323
  53.5 2.7 %solve.1 = f32[512,128]{1,0:T(8,128)S(1)} custom-call(f32[2080]{0:T(1024)S(1)} %copy-done.9, f32[16,16,128]{2,1,0:T(8,128)S(1)} %get-tuple-element.34.cx, f32[16,16,128]{2,1,0:T(8,128)S(1)} %get-tuple-element.35.cyp, f32[16,16,128]{2,1,0:T(8,128)S(1)} %get-tuple-element.36.cym, f32[16,16,128]{2,1,0:T(8,128)S(1)} %get-tuple-element.37.czp, ...), custom_call_target="tpu_custom_call" | custom-call | tf_op jit(solution)/shard_map/solve/pallas_call | solution.py:324
  56.2 0.0 copy-start.6
  56.2 0.0 copy-start.7
  56.2 0.0 copy-start.8
  56.3 20.4 %all_to_all.39 = f32[256,2,128]{2,1,0:T(2,128)S(1)} all-to-all(f32[256,2,128]{2,1,0:T(2,128)S(1)} %bitcast.17), channel_id=1, replica_groups=mesh['tm'=64,'space'=4] {'space','tm'}, dimensions={0} | all-to-all | bytes 524288 | tf_op jit(solution)/shard_map/all_to_all | solution.py:333
  76.6 0.3 inverse.1
  76.9 0.0 copy-start
  76.9 0.0 copy-start.1
  76.9 14.6 %all_to_all.40 = f32[64,4,128]{2,1,0:T(4,128)S(1)} all-to-all(f32[64,4,128]{2,1,0:T(4,128)S(1)} %bitcast.20), channel_id=1, replica_groups=mesh['tm'=64,'space'=4] {'tm'}, dimensions={0} | all-to-all | bytes 262144 | tf_op jit(solution)/shard_map/all_to_all | solution.py:342
  91.5 0.0 copy-done
  91.6 0.7 update.1
  (5 shorter events, 0.0 us)
Async XLA Ops:
  2.3 12.7 %copy-start.2 = (f32[2,4,16,128]{3,2,1,0:T(8,128)S(1)}, f32[2,4,16,128]{3,2,1,0:T(8,128)}, u32[]{:S(2)}) copy-start(f32[2,4,16,128]{3,2,1,0:T(8,128)} %get-tuple-element.24.m0_ref) | copy-start | bytes 196612
  2.3 25.2 %copy-start.3 = (f32[4,16,128]{2,1,0:T(8,128)S(1)}, f32[4,16,128]{2,1,0:T(8,128)}, u32[]{:S(2)}) copy-start(f32[4,16,128]{2,1,0:T(8,128)} %param.13) | copy-start | bytes 98308
  2.3 25.2 %copy-start.4 = (bf16[128,128]{1,0:T(8,128)(2,1)S(1)}, bf16[128,128]{1,0:T(8,128)(2,1)}, u32[]{:S(2)}) copy-start(bf16[128,128]{1,0:T(8,128)(2,1)} %constant.22.fl_ref) | copy-start | bytes 98308
  2.3 25.1 %copy-start.5 = (bf16[128,128]{1,0:T(8,128)(2,1)S(1)}, bf16[128,128]{1,0:T(8,128)(2,1)}, u32[]{:S(2)}) copy-start(bf16[128,128]{1,0:T(8,128)(2,1)} %constant.19.fh_ref) | copy-start | bytes 98308
  2.3 22.9 %all-to-all-start = ((f32[192,2,128]{2,1,0:T(2,128)}), f32[192,2,128]{2,1,0:T(2,128)S(1)}, u32[]{:S(2)}, u32[]{:S(2)}) async-start(f32[192,2,128]{2,1,0:T(2,128)} %bitcast.26), calls=%async_computation | async-start | bytes 393216 | tf_op jit(solution)/shard_map/all_to_all | solution.py:297
  15.0 8.6 %collective-permute-start = (f32[2,4,16,128]{3,2,1,0:T(8,128)S(1)}, f32[2,4,16,128]{3,2,1,0:T(8,128)S(1)}, u32[]{:S(2)}, u32[]{:S(2)}) collective-permute-start(f32[2,4,16,128]{3,2,1,0:T(8,128)S(1)} %copy-done.2), channel_id=1, source_target_pairs={{0,2},{1,3},{2,0},{3,1},{4,6},{5,7},{6,4},{7,5},{8,10},{9,11},{10,... | collective-permute-start | bytes 196616 | tf_op jit(solution)/shard_map/ppermute | solution.py:265
  19.3 8.4 %collective-permute-start.1 = (f32[2,4,16,128]{3,2,1,0:T(8,128)S(1)}, f32[2,4,16,128]{3,2,1,0:T(8,128)S(1)}, u32[]{:S(2)}, u32[]{:S(2)}) collective-permute-start(f32[2,4,16,128]{3,2,1,0:T(8,128)S(1)} %copy-done.2), channel_id=1, source_target_pairs={{0,1},{1,0},{2,3},{3,2},{4,5},{5,4},{6,7},{7,6},{8,9},{9,8},{10,11... | collective-permute-start | bytes 196616 | tf_op jit(solution)/shard_map/ppermute | solution.py:265
  25.3 3.1 %collective-permute-start.2 = (f32[2,4,16,128]{3,2,1,0:T(8,128)S(1)}, f32[2,4,16,128]{3,2,1,0:T(8,128)S(1)}, u32[]{:S(2)}, u32[]{:S(2)}) collective-permute-start(f32[2,4,16,128]{3,2,1,0:T(8,128)S(1)} %collective-permute-done.m2_ref), channel_id=1, source_target_pairs={{0,1},{1,0},{2,3},{3,2},{4,5},{5,4},{6,7},{7,6},{8,9},{9,8},{10,11... | collective-permute-start | bytes 196616 | tf_op jit(solution)/shard_map/ppermute | solution.py:265
  28.5 25.0 %copy-start.9 = (f32[2080]{0:T(1024)S(1)}, f32[2080]{0:T(1024)}, u32[]{:S(2)}) copy-start(f32[2080]{0:T(1024)} %constant.10.clone.co_ref) | copy-start | bytes 24964
  56.2 20.4 %copy-start.6 = (bf16[128,128]{1,0:T(8,128)(2,1)S(1)}, bf16[128,128]{1,0:T(8,128)(2,1)}, u32[]{:S(2)}) copy-start(bf16[128,128]{1,0:T(8,128)(2,1)} %constant.18.gl_ref) | copy-start | bytes 98308
  56.2 20.4 %copy-start.7 = (bf16[128,128]{1,0:T(8,128)(2,1)S(1)}, bf16[128,128]{1,0:T(8,128)(2,1)}, u32[]{:S(2)}) copy-start(bf16[128,128]{1,0:T(8,128)(2,1)} %constant.15.gh_ref) | copy-start | bytes 98308
  56.2 20.4 %copy-start.8 = (f32[64,128]{1,0:T(8,128)S(1)}, f32[64,128]{1,0:T(8,128)}, u32[]{:S(2)}) copy-start(f32[64,128]{1,0:T(8,128)} %constant.11.clone.b_ref) | copy-start | bytes 98308
  76.9 14.6 %copy-start = (f32[2,4,16,128]{3,2,1,0:T(8,128)S(1)}, f32[2,4,16,128]{3,2,1,0:T(8,128)}, u32[]{:S(2)}) copy-start(f32[2,4,16,128]{3,2,1,0:T(8,128)} %param.10) | copy-start | bytes 196612
  76.9 14.6 %copy-start.1 = (f32[2,4,16,128]{3,2,1,0:T(8,128)S(1)}, f32[2,4,16,128]{3,2,1,0:T(8,128)}, u32[]{:S(2)}) copy-start(f32[2,4,16,128]{3,2,1,0:T(8,128)} %param.11) | copy-start | bytes 196612

commit v4 on v3

--- a/solution.py
+++ b/solution.py
@@ -51,16 +51,22 @@
     centre = 0.5 * (upper + lower)
     half = 0.5 * (upper - lower)
     ratio = centre / half
-    rho = 1.0 / ratio
+    gamma = np.sqrt(2.0 / half)
+    offset = np.sqrt(2.0 * (centre - spread) / half)
     table = np.zeros((slots + 1, COEF))
-    table[:, 0] = shift
-    table[:, 1] = spread
-    table[:, 2] = 1.0 / centre
-    for step in range(CHEB - 1):
-        rho_next = 1.0 / (2.0 * ratio - rho)
-        table[:, 4 + 2 * step] = rho_next * rho
-        table[:, 5 + 2 * step] = 2.0 * rho_next / half
-        rho = rho_next
+    table[:, 0] = gamma
+    table[:, 1] = offset
+    table[:, 2] = shift
+    table[:, 3] = 1.0 / gamma
+    table[:, 4] = offset / gamma
+    nodes = np.pi * (np.arange(CHEB) + 0.5) / CHEB
+    points = np.cos(nodes)[None, :]
+    value = centre[:, None] + half[:, None] * points
+    top = np.cosh(CHEB * np.arccosh(ratio))[:, None]
+    samples = (1.0 - np.cos(CHEB * np.arccos(-points)) / top) / value
+    for j in range(CHEB):
+        weight = (1.0 if j == 0 else 2.0) / CHEB
+        table[:, 8 + j] = weight * np.sum(samples * np.cos(j * nodes)[None, :], 1)
     return table.reshape(-1).astype(np.float32), twist[:slots]
 
 
@@ -139,95 +145,175 @@
                 ]
 
 
-def faces_kernel(m0_ref, m1_ref, m2_ref, m3_ref, cx, cyp, cym, czp, czm, bare, both, mat):
+def coefficients(slots):
+    slot = lax.axis_index("tm")
     item = lax.axis_index("space")
+    return item, jnp.where((slot == 0) & (item % 2 == 1), slots, slot) * COEF
+
+
+def faces_kernel(
+    slots,
+    co_ref,
+    m0_ref,
+    m1_ref,
+    m2_ref,
+    m3_ref,
+    cx,
+    cy,
+    cy_next,
+    cy_last,
+    cz_next,
+    cz_last,
+    bare,
+    plus,
+    minus,
+    mat,
+):
+    item, base = coefficients(slots)
+    gamma = co_ref[base]
+    offset = co_ref[base + 1]
+    shift = co_ref[base + 2]
     for piece, ref in enumerate((m0_ref, m1_ref, m2_ref, m3_ref)):
         mat[item ^ piece] = ref[...]
-    slabs, _, width, count_y, lanes = mat.shape
-    count = slabs * width
-    row = lax.broadcasted_iota(jnp.int32, (count_y, lanes), 0)
-    lane = lax.broadcasted_iota(jnp.int32, (count_y, lanes), 1)
-
-    def cond(x):
-        return mat[x // width, 0, x % width]
+    count, _, subs, lanes = cx.shape
+    width = mat.shape[2]
+    sub = lax.broadcasted_iota(jnp.int32, (subs, lanes), 0)
+    lane = lax.broadcasted_iota(jnp.int32, (subs, lanes), 1)
+    first, last = sub == 0, sub == subs - 1
+    left, right = lane == 0, lane == lanes - 1
+
+    def part(which, x, parity):
+        return mat.at[x // width, which, x % width][rows_of(subs, parity, 2), :]
 
     for x in range(count):
-        c = cond(x)
-        half = 0.5 * c
-        up = 0.5 * (c + cond(x + 1)) if x + 1 < count else half
-        down = 0.5 * (c + cond(x - 1)) if x > 0 else half
-        cx[x] = up
-        yp = jnp.where(row == count_y - 1, 0.0, 0.5 * pltpu.roll(c, count_y - 1, 0)) + half
-        ym = jnp.where(row == 0, 0.0, 0.5 * pltpu.roll(c, 1, 0)) + half
-        zp = jnp.where(lane == lanes - 1, 0.0, 0.5 * pltpu.roll(c, lanes - 1, 1)) + half
-        zm = jnp.where(lane == 0, 0.0, 0.5 * pltpu.roll(c, 1, 1)) + half
-        total = (up + down) + (yp + ym) + (zp + zm)
-        bare[x] = total
-        both[x] = total + mat[x // width, 1, x % width]
-        cyp[x] = jnp.where(row == count_y - 1, 0.0, yp)
-        cym[x] = jnp.where(row == 0, 0.0, ym)
-        czp[x] = jnp.where(lane == lanes - 1, 0.0, zp)
-        czm[x] = jnp.where(lane == 0, 0.0, zm)
-
-
-def solve_kernel(co_ref, cx, cyp, cym, czp, czm, bare, both, x_ref, o_ref, diag, yy, res, d, t, w):
-    slot = lax.axis_index("tm")
-    item = lax.axis_index("space")
+        even, odd = part(0, x, 0), part(0, x, 1)
+        pair = 0.5 * (even + odd)
+        after = 0.5 * odd + jnp.where(last, 0.0, 0.5 * pltpu.roll(even, subs - 1, 0))
+        before = 0.5 * even + jnp.where(first, 0.0, 0.5 * pltpu.roll(odd, 1, 0))
+        cy[x] = gamma * pair
+        cy_next[x] = gamma * jnp.where(last, 0.0, after)
+        cy_last[x] = gamma * jnp.where(first, 0.0, before)
+        for parity, (c, side) in enumerate(((even, before), (odd, after))):
+            half = 0.5 * c
+            up = half + 0.5 * part(0, x + 1, parity) if x + 1 < count else half
+            down = half + 0.5 * part(0, x - 1, parity) if x > 0 else half
+            zn = half + jnp.where(right, 0.0, 0.5 * pltpu.roll(c, lanes - 1, 1))
+            zl = half + jnp.where(left, 0.0, 0.5 * pltpu.roll(c, 1, 1))
+            cx[x, parity] = gamma * up
+            cz_next[x, parity] = gamma * jnp.where(right, 0.0, zn)
+            cz_last[x, parity] = gamma * jnp.where(left, 0.0, zl)
+            total = (up + down) + (pair + side) + (zn + zl)
+            bare[x, parity] = gamma * total
+            full = gamma * (total + part(1, x, parity) + shift)
+            plus[x, parity] = full + offset
+            minus[x, parity] = full - offset
+
+
+def solve_kernel(
+    slots,
+    co_ref,
+    cx,
+    cy,
+    cy_next,
+    cy_last,
+    cz_next,
+    cz_last,
+    bare,
+    plus,
+    minus,
+    x_ref,
+    o_ref,
+    res,
+    b0,
+    b1,
+    t,
+):
+    base = coefficients(slots)[1]
+    count, _, subs, lanes = cx.shape
     cells = x_ref.shape[0] // 8
-    slots = cells
-    frequency = jnp.where((slot == 0) & (item % 2 == 1), slots, slot)
-    base = frequency * COEF
-    shift = co_ref[base]
-    spread = co_ref[base + 1]
-    start = co_ref[base + 2]
-    slabs = 4
-    count, count_y, lanes = d.shape
-    width = count // slabs
-    for s in range(slabs):
-        res[s * width : (s + 1) * width] = x_ref[rows_of(cells, 2 * s * cells, 2), :].reshape(width, count_y, lanes)
-        yy[s * width : (s + 1) * width] = x_ref[rows_of(cells, 2 * s * cells + 1, 2), :].reshape(width, count_y, lanes)
-
-    def applied(ref, x, centre):
-        v = ref[x]
-        out = centre * v
-        if x + 1 < count:
-            out = out - cx[x] * ref[x + 1]
-        if x > 0:
-            out = out - cx[x - 1] * ref[x - 1]
-        out = out - cyp[x] * pltpu.roll(v, count_y - 1, 0)
-        out = out - cym[x] * pltpu.roll(v, 1, 0)
-        out = out - czp[x] * pltpu.roll(v, lanes - 1, 1)
-        out = out - czm[x] * pltpu.roll(v, 1, 1)
-        return out
-
-    for x in range(count):
-        diag[x] = both[x] + shift
-        r = res[x] + applied(yy, x, bare[x])
-        first = start * r
-        res[x] = r
-        d[x] = first
-        w[x] = first
-
-    def step(i, carry):
-        alpha = co_ref[base + 4 + 2 * i]
-        beta = co_ref[base + 5 + 2 * i]
+    line = 2 * subs
+    width = cells // line
+
+    def place(x, parity, field):
+        start = (x // width * cells + x % width * line + parity) * 2 + field
+        return rows_of(subs, start, 4)
+
+    def sweep(load, diag, emit):
+        now, cx_now = load(0), None
+        last = cx_last = None
         for x in range(count):
-            t[x] = applied(d, x, diag[x])
-        for x in range(count):
-            now = d[x]
-            r = res[x] - (applied(t, x, diag[x]) + spread * now)
-            now = alpha * now + beta * r
-            res[x] = r
-            d[x] = now
-            w[x] = w[x] + now
+            after = load(x + 1) if x + 1 < count else None
+            cx_now = (cx[x, 0], cx[x, 1]) if x + 1 < count else None
+            pair = cy[x]
+            side = (
+                pair * now[1] + cy_last[x] * pltpu.roll(now[1], 1, 0),
+                pair * now[0] + cy_next[x] * pltpu.roll(now[0], subs - 1, 0),
+            )
+            for parity in range(2):
+                v = now[parity]
+                out = diag[x, parity] * v - side[parity]
+                lateral = cz_next[x, parity] * pltpu.roll(v, lanes - 1, 1)
+                lateral = lateral + cz_last[x, parity] * pltpu.roll(v, 1, 1)
+                if after is not None:
+                    out = out - cx_now[parity] * after[parity]
+                if last is not None:
+                    lateral = lateral + cx_last[parity] * last[parity]
+                emit(x, parity, out - lateral, v)
+            last, now, cx_last = now, after, cx_now
+
+    def kept(ref):
+        return lambda x: (ref[x, 0], ref[x, 1])
+
+    inverse_gamma = co_ref[base + 3]
+    top = co_ref[base + 8 + CHEB - 1]
+
+    def begin(x, parity, out, v):
+        r = x_ref[place(x, parity, 0), :] + inverse_gamma * out
+        res[x, parity] = r
+        b0[x, parity] = top * r
+        b1[x, parity] = jnp.zeros_like(r)
+
+    sweep(
+        lambda x: (x_ref[place(x, 0, 1), :], x_ref[place(x, 1, 1), :]),
+        bare,
+        begin,
+    )
+
+    def first_factor(source):
+        def keep(x, parity, out, v):
+            t[x, parity] = out
+
+        sweep(kept(source), plus, keep)
+
+    def clenshaw(source, target, weight):
+        def keep(x, parity, out, v):
+            target[x, parity] = (weight * res[x, parity] - target[x, parity]) + out
+
+        first_factor(source)
+        sweep(kept(t), minus, keep)
+
+    def two_steps(i, carry):
+        at = base + 8 + CHEB - 2 - 2 * i
+        clenshaw(b0, b1, co_ref[at])
+        clenshaw(b1, b0, co_ref[at - 1])
         return carry
 
-    lax.fori_loop(0, CHEB - 1, step, 0)
-    for x in range(count):
-        t[x] = applied(w, x, diag[x])
-    for s in range(slabs):
-        o_ref[rows_of(cells, 2 * s * cells, 2), :] = w[s * width : (s + 1) * width].reshape(width * count_y, lanes)
-        o_ref[rows_of(cells, 2 * s * cells + 1, 2), :] = t[s * width : (s + 1) * width].reshape(width * count_y, lanes)
+    lax.fori_loop(0, (CHEB - 2) // 2, two_steps, 0)
+    weight = co_ref[base + 8]
+    offset = co_ref[base + 4]
+
+    def finish(x, parity, out, v):
+        w = (weight * res[x, parity] - b1[x, parity]) + 0.5 * out
+        b1[x, parity] = w
+        o_ref[place(x, parity, 0), :] = w
+
+    first_factor(b0)
+    sweep(kept(t), minus, finish)
+
+    def image(x, parity, out, v):
+        o_ref[place(x, parity, 1), :] = inverse_gamma * out - offset * v
+
+    sweep(kept(b1), plus, image)
 
 
 def inverse_kernel(gh_ref, gl_ref, b_ref, x_ref, o_ref):
@@ -308,25 +394,26 @@
         compiler_params=grant,
         name="forward",
     )(*forward, initial_state.reshape(rows, width_z), by_cell)
-    grid = (spaces * width_x, width_y, width_z)
+    grid = (spaces * width_x, 2, width_y // 2, width_z)
+    pairs = (spaces * width_x, width_y // 2, width_z)
     faces = pl.pallas_call(
-        faces_kernel,
-        out_shape=(shape(*grid),) * 7,
-        in_specs=[vmem()] * 4,
-        out_specs=(vmem(),) * 7,
+        functools.partial(faces_kernel, devices),
+        out_shape=(shape(*grid),) + (shape(*pairs),) * 3 + (shape(*grid),) * 5,
+        in_specs=[smem()] + [vmem()] * 4,
+        out_specs=(vmem(),) * 9,
         scratch_shapes=[pltpu.VMEM((spaces, 2, width_x, width_y, width_z), f32)],
         compiler_params=grant,
         name="faces",
-    )(material, material_core, material_far, material_both)
+    )(jnp.asarray(table), material, material_core, material_far, material_both)
     hat, faces = lax.optimization_barrier((hat, faces))
     everyone = ("space", "tm")
     by_item = lax.all_to_all(hat, everyone, 0, 0, tiled=True)
     solved = pl.pallas_call(
-        solve_kernel,
+        functools.partial(solve_kernel, devices),
         out_shape=shape(rows * 8, width_z),
-        in_specs=[smem()] + [vmem()] * 8,
+        in_specs=[smem()] + [vmem()] * 10,
         out_specs=vmem(),
-        scratch_shapes=[pltpu.VMEM(grid, f32)] * 6,
+        scratch_shapes=[pltpu.VMEM(grid, f32)] * 4,
         compiler_params=grant,
         name="solve",
     )(jnp.asarray(table), *faces, by_item)

time: 92.7 us -> 92.9 us (level)
  no operation moved by 1% of the time
where the time goes in v4:
time: 92.9 us; the launch traced here: 92.5 us
  blocking collectives  59.9 us (64%)
  starting transfers between devices  20.4 us (22%)
  Pallas kernels  6.05 us (7%)
  waiting for transfers between devices  5.3 us (6%)
    all_to_all x1, blocking collectives, shards(): by_item = lax.all_to_all(hat, everyone, 0, 0, tiled=True)  24.9 us
    all_to_all x1, blocking collectives, shards(): by_row = lax.all_to_all(solved, everyone, 0, 0, tiled=True)  20.4 us
    all_to_all x1, blocking collectives, shards(): by_time = lax.all_to_all(delta, 'tm', 0, 0, tiled=True)  14.6 us
    all_to_all x1, starting transfers between devices, shards(): lax.all_to_all(packed.reshape(rows * 3, 2, width_z), 'tm', 0, 0, tiled=True)  12.7 us
    ppermute x3, starting transfers between devices, swapped(): lax.ppermute(value, 'space', [(i, i ^ distance) for i in range(count)])  7.74 us
    ppermute x3, waiting for transfers between devices, swapped(): lax.ppermute(value, 'space', [(i, i ^ distance) for i in range(count)])  3.68 us
    pallas_call x1, Pallas kernels, shards(): pl.pallas_call(functools.partial(solve_kernel, devices), out_shape=shape(...  2.33 us
  transfers between devices with their start and end apart: 4, of which 3 were waited for; matrix products, arithmetic and copies ran while one was open for 0% of the time, Pallas kernels for 0%

profile of v4, /device:TPU:1, one launch (start us, length us, event | category | flops | bytes accessed | tf_op | source)
XLA Modules:
  0.0 92.5 jit_solution(17601741816419433939)
XLA Ops:
  0.6 1.6 %pack.1 = (f32[384,128]{1,0:T(8,128)}, f32[2,4,16,128]{3,2,1,0:T(8,128)}) custom-call(f32[4,16,128]{2,1,0:T(8,128)} %c_hbm.1, f32[4,16,128]{2,1,0:T(8,128)} %r_hbm.1, f32[2,64,128]{2,1,0:T(8,128)} %bitcast.21, f32[2,64,128]{2,1,0:T(8,128)} %bitcast.23, f32[2,64,128]{2,1,0:T(8,128)} %bitcast.27), custom_call_target="tpu_custom_call" | custom-call | tf_op jit(solution)/shard_map/pack/pallas_call | solution.py:369
  2.3 0.0 copy-start.2
  2.3 0.0 copy-start.4
  2.3 0.0 copy-start.5
  2.3 0.0 copy-start.6
  2.3 12.7 %all-to-all-start = ((f32[192,2,128]{2,1,0:T(2,128)}), f32[192,2,128]{2,1,0:T(2,128)S(1)}, u32[]{:S(2)}, u32[]{:S(2)}) async-start(f32[192,2,128]{2,1,0:T(2,128)} %bitcast.26), calls=%async_computation | async-start | bytes 393216 | tf_op jit(solution)/shard_map/all_to_all | solution.py:383
  15.0 0.0 copy-done.2
  15.0 4.3 %collective-permute-start = (f32[2,4,16,128]{3,2,1,0:T(8,128)S(1)}, f32[2,4,16,128]{3,2,1,0:T(8,128)S(1)}, u32[]{:S(2)}, u32[]{:S(2)}) collective-permute-start(f32[2,4,16,128]{3,2,1,0:T(8,128)S(1)} %copy-done.2), channel_id=1, source_target_pairs={{0,2},{1,3},{2,0},{3,1},{4,6},{5,7},{6,4},{7,5},{8,10},{9,11},{10,... | collective-permute-start | bytes 196616 | tf_op jit(solution)/shard_map/ppermute | solution.py:351
  19.3 1.2 %collective-permute-start.1 = (f32[2,4,16,128]{3,2,1,0:T(8,128)S(1)}, f32[2,4,16,128]{3,2,1,0:T(8,128)S(1)}, u32[]{:S(2)}, u32[]{:S(2)}) collective-permute-start(f32[2,4,16,128]{3,2,1,0:T(8,128)S(1)} %copy-done.2), channel_id=1, source_target_pairs={{0,1},{1,0},{2,3},{3,2},{4,5},{5,4},{6,7},{7,6},{8,9},{9,8},{10,11... | collective-permute-start | bytes 196616 | tf_op jit(solution)/shard_map/ppermute | solution.py:351
  20.6 3.1 %collective-permute-done.m2_ref = f32[2,4,16,128]{3,2,1,0:T(8,128)S(1)} collective-permute-done((f32[2,4,16,128]{3,2,1,0:T(8,128)S(1)}, f32[2,4,16,128]{3,2,1,0:T(8,128)S(1)}, u32[]{:S(2)}, u32[]{:S(2)}) %collective-permute-start) | collective-permute-done | bytes 65568 | tf_op jit(solution)/shard_map/ppermute | solution.py:351
  23.6 1.6 %all-to-all-done = f32[192,2,128]{2,1,0:T(2,128)S(1)} async-done(((f32[192,2,128]{2,1,0:T(2,128)}), f32[192,2,128]{2,1,0:T(2,128)S(1)}, u32[]{:S(2)}, u32[]{:S(2)}) %all-to-all-start) | async-done | bytes 196640 | tf_op jit(solution)/shard_map/all_to_all | solution.py:383
  25.3 2.2 %collective-permute-start.2 = (f32[2,4,16,128]{3,2,1,0:T(8,128)S(1)}, f32[2,4,16,128]{3,2,1,0:T(8,128)S(1)}, u32[]{:S(2)}, u32[]{:S(2)}) collective-permute-start(f32[2,4,16,128]{3,2,1,0:T(8,128)S(1)} %collective-permute-done.m2_ref), channel_id=1, source_target_pairs={{0,1},{1,0},{2,3},{3,2},{4,5},{5,4},{6,7},{7,6},{8,9},{9,8},{10,11... | collective-permute-start | bytes 196616 | tf_op jit(solution)/shard_map/ppermute | solution.py:351
  27.5 0.0 copy-done.4
  27.5 0.0 copy-done.5
  27.5 0.0 copy-done.6
  27.5 0.3 forward.1
  27.7 0.0 collective-permute-done.1.m1_ref
  27.7 0.6 collective-permute-done.2.m3_ref
  28.4 0.0 copy-done.3
  28.4 0.9 faces.1
  29.2 24.9 %all_to_all.38 = f32[256,2,128]{2,1,0:T(2,128)S(1)} all-to-all(f32[256,2,128]{2,1,0:T(2,128)S(1)} %bitcast.14), channel_id=1, replica_groups=mesh['tm'=64,'space'=4] {'space','tm'}, dimensions={0} | all-to-all | bytes 524288 | tf_op jit(solution)/shard_map/all_to_all | solution.py:410
  54.2 2.3 %solve.1 = f32[512,128]{1,0:T(8,128)S(1)} custom-call(f32[2080]{0:T(1024)S(1)} %copy-done.3, f32[16,2,8,128]{3,2,1,0:T(8,128)S(1)} %get-tuple-element.40.cx, f32[16,8,128]{2,1,0:T(8,128)S(1)} %get-tuple-element.41.cy, f32[16,8,128]{2,1,0:T(8,128)S(1)} %get-tuple-element.42.cy_next, f32[16,8,128]{2,1,0:T(8,128)S(1)} %get-tuple-element.43.cy_last, ...), custom_call_target="tpu_custom_call" | custom-call | tf_op jit(solution)/shard_map/solve/pallas_call | solution.py:411
  56.5 0.0 copy-start.7
  56.5 0.0 copy-start.8
  56.6 0.0 copy-start.9
  56.6 20.4 %all_to_all.39 = f32[256,2,128]{2,1,0:T(2,128)S(1)} all-to-all(f32[256,2,128]{2,1,0:T(2,128)S(1)} %bitcast.17), channel_id=1, replica_groups=mesh['tm'=64,'space'=4] {'space','tm'}, dimensions={0} | all-to-all | bytes 524288 | tf_op jit(solution)/shard_map/all_to_all | solution.py:420
  76.9 0.0 copy-done.7
  76.9 0.3 inverse.1
  77.2 0.0 copy-start
  77.2 0.0 copy-start.1
  77.3 14.6 %all_to_all.40 = f32[64,4,128]{2,1,0:T(4,128)S(1)} all-to-all(f32[64,4,128]{2,1,0:T(4,128)S(1)} %bitcast.20), channel_id=1, replica_groups=mesh['tm'=64,'space'=4] {'tm'}, dimensions={0} | all-to-all | bytes 262144 | tf_op jit(solution)/shard_map/all_to_all | solution.py:429
  91.9 0.7 update.1
  (5 shorter events, 0.0 us)
Async XLA Ops:
  2.3 12.7 %copy-start.2 = (f32[2,4,16,128]{3,2,1,0:T(8,128)S(1)}, f32[2,4,16,128]{3,2,1,0:T(8,128)}, u32[]{:S(2)}) copy-start(f32[2,4,16,128]{3,2,1,0:T(8,128)} %get-tuple-element.28.m0_ref) | copy-start | bytes 196612
  2.3 25.2 %copy-start.4 = (f32[4,16,128]{2,1,0:T(8,128)S(1)}, f32[4,16,128]{2,1,0:T(8,128)}, u32[]{:S(2)}) copy-start(f32[4,16,128]{2,1,0:T(8,128)} %param.13) | copy-start | bytes 98308
  2.3 25.2 %copy-start.5 = (bf16[128,128]{1,0:T(8,128)(2,1)S(1)}, bf16[128,128]{1,0:T(8,128)(2,1)}, u32[]{:S(2)}) copy-start(bf16[128,128]{1,0:T(8,128)(2,1)} %constant.22.fl_ref) | copy-start | bytes 98308
  2.3 25.1 %copy-start.6 = (bf16[128,128]{1,0:T(8,128)(2,1)S(1)}, bf16[128,128]{1,0:T(8,128)(2,1)}, u32[]{:S(2)}) copy-start(bf16[128,128]{1,0:T(8,128)(2,1)} %constant.19.fh_ref) | copy-start | bytes 98308
  2.3 22.9 %all-to-all-start = ((f32[192,2,128]{2,1,0:T(2,128)}), f32[192,2,128]{2,1,0:T(2,128)S(1)}, u32[]{:S(2)}, u32[]{:S(2)}) async-start(f32[192,2,128]{2,1,0:T(2,128)} %bitcast.26), calls=%async_computation | async-start | bytes 393216 | tf_op jit(solution)/shard_map/all_to_all | solution.py:383
  15.0 8.6 %collective-permute-start = (f32[2,4,16,128]{3,2,1,0:T(8,128)S(1)}, f32[2,4,16,128]{3,2,1,0:T(8,128)S(1)}, u32[]{:S(2)}, u32[]{:S(2)}) collective-permute-start(f32[2,4,16,128]{3,2,1,0:T(8,128)S(1)} %copy-done.2), channel_id=1, source_target_pairs={{0,2},{1,3},{2,0},{3,1},{4,6},{5,7},{6,4},{7,5},{8,10},{9,11},{10,... | collective-permute-start | bytes 196616 | tf_op jit(solution)/shard_map/ppermute | solution.py:351
  19.3 8.4 %collective-permute-start.1 = (f32[2,4,16,128]{3,2,1,0:T(8,128)S(1)}, f32[2,4,16,128]{3,2,1,0:T(8,128)S(1)}, u32[]{:S(2)}, u32[]{:S(2)}) collective-permute-start(f32[2,4,16,128]{3,2,1,0:T(8,128)S(1)} %copy-done.2), channel_id=1, source_target_pairs={{0,1},{1,0},{2,3},{3,2},{4,5},{5,4},{6,7},{7,6},{8,9},{9,8},{10,11... | collective-permute-start | bytes 196616 | tf_op jit(solution)/shard_map/ppermute | solution.py:351
  25.3 3.1 %collective-permute-start.2 = (f32[2,4,16,128]{3,2,1,0:T(8,128)S(1)}, f32[2,4,16,128]{3,2,1,0:T(8,128)S(1)}, u32[]{:S(2)}, u32[]{:S(2)}) collective-permute-start(f32[2,4,16,128]{3,2,1,0:T(8,128)S(1)} %collective-permute-done.m2_ref), channel_id=1, source_target_pairs={{0,1},{1,0},{2,3},{3,2},{4,5},{5,4},{6,7},{7,6},{8,9},{9,8},{10,11... | collective-permute-start | bytes 196616 | tf_op jit(solution)/shard_map/ppermute | solution.py:351
  27.5 0.9 copy-start.3
  56.5 20.4 %copy-start.7 = (bf16[128,128]{1,0:T(8,128)(2,1)S(1)}, bf16[128,128]{1,0:T(8,128)(2,1)}, u32[]{:S(2)}) copy-start(bf16[128,128]{1,0:T(8,128)(2,1)} %constant.18.gl_ref) | copy-start | bytes 98308
  56.5 20.4 %copy-start.8 = (bf16[128,128]{1,0:T(8,128)(2,1)S(1)}, bf16[128,128]{1,0:T(8,128)(2,1)}, u32[]{:S(2)}) copy-start(bf16[128,128]{1,0:T(8,128)(2,1)} %constant.15.gh_ref) | copy-start | bytes 98308
  56.6 20.4 %copy-start.9 = (f32[64,128]{1,0:T(8,128)S(1)}, f32[64,128]{1,0:T(8,128)}, u32[]{:S(2)}) copy-start(f32[64,128]{1,0:T(8,128)} %constant.11.clone.b_ref) | copy-start | bytes 98308
  77.2 14.6 %copy-start = (f32[2,4,16,128]{3,2,1,0:T(8,128)S(1)}, f32[2,4,16,128]{3,2,1,0:T(8,128)}, u32[]{:S(2)}) copy-start(f32[2,4,16,128]{3,2,1,0:T(8,128)} %param.10) | copy-start | bytes 196612
  77.2 14.6 %copy-start.1 = (f32[2,4,16,128]{3,2,1,0:T(8,128)S(1)}, f32[2,4,16,128]{3,2,1,0:T(8,128)}, u32[]{:S(2)}) copy-start(f32[2,4,16,128]{3,2,1,0:T(8,128)} %param.11) | copy-start | bytes 196612
